TPU v7x, 256 devices: a whole 4x4x8 slice. The times are simulated.
256 devices in a mesh: region: 32 (over z, x_hi, core), member: 8 (over y, x_lo).
Axes of the slice: x: 4 (x_hi: 2, x_lo: 2; x = x_hi * 2 + x_lo), y: 4, z: 8, core: 2. Of those that a mesh axis runs over, the one named last changes fastest.
Arguments:
- state: float32 [1024, 256, 256], P('member', 'region'), may hold values from -8 to 8
- neighbours: int32 [256, 5], replicated, may hold values from 0 to 255, as said below
- obs_cell: int32 [256, 2, 64], replicated, may hold values from 0 to 255
- obs_values: float32 [256, 2, 64], replicated, may hold values from -6 to 6
- obs_var: float32 [256, 2, 64], replicated, may hold values from 0.25 to 1
Outputs:
- analysis: float32 [1024, 256, 256], P('member', 'region')
Inputs may be any that keep to these rules, and one draw needn't show every extreme that they name: `neighbours`: patch g lies in region g // 8. Each patch lists 5 different patches in some order: two of the region before its own and two of the region after it (regions wrap around), and one other patch of its own region.
All inputs are finite; a program needn't handle non-finite values.
Results may differ from a plain program's by a relative error of at most 0.0003.
Values sent between devices are 32-bit elements; how exact they have to be, the bound alone decides.
A program may use at most 128 MiB of HBM per device.

v0:
```python
import jax
import jax.numpy as jnp
from jax import lax
from jax.sharding import PartitionSpec as P

NBATCH = 2


HIGHEST = lax.Precision.HIGHEST


def joined_along(blocks, dim):
    blocks = jnp.moveaxis(blocks, 0, dim)
    shape = blocks.shape
    return blocks.reshape(*shape[:dim], shape[dim] * shape[dim + 1], *shape[dim + 2 :])


def sent_to_all(x, axis):
    copies = jnp.broadcast_to(x, (lax.axis_size(axis), *x.shape))
    return lax.all_to_all(copies, axis, split_axis=0, concat_axis=0, tiled=True)


def collect(x, axis, dim):
    return joined_along(sent_to_all(x, axis), dim)


def with_halo(x, sides, width):
    for axis, dim in sides:
        size, length = (lax.axis_size(axis), x.shape[dim])
        up = [(i, (i + 1) % size) for i in range(size)]
        down = [(j, i) for i, j in up]
        last = lax.slice_in_dim(x, length - width, length, axis=dim)
        leading = lax.slice_in_dim(x, 0, width, axis=dim)
        before = lax.ppermute(last, axis, up)
        after = lax.ppermute(leading, axis, down)
        x = jnp.concatenate([before, x, after], axis=dim)
    return x


def analyse(stacked, values, variances, patch_state):
    members = stacked.shape[1]
    obs_mean = jnp.mean(stacked, axis=1)
    spread = stacked - obs_mean[:, None]
    innovation = values - obs_mean
    covariance = jnp.dot(spread, spread.T, precision=HIGHEST) / (members - 1.0) + jnp.diag(
        variances
    )
    state_mean = jnp.mean(patch_state, axis=0)
    anomaly = patch_state - state_mean[None, :]
    cross_cov = jnp.dot(spread, anomaly, precision=HIGHEST)
    factor = jnp.linalg.cholesky(covariance)
    kalman_gain = jax.scipy.linalg.cho_solve((factor, True), cross_cov) / (members - 1.0)
    combined = innovation[:, None] - 0.5 * spread
    update = lax.dot_general(combined, kalman_gain, (((0,), (0,)), ((), ())), precision=HIGHEST)
    return patch_state + update


def on_device(state, neighbours, obs_cell, obs_values, obs_var):
    ensemble = lax.all_to_all(state, "member", split_axis=1, concat_axis=0, tiled=True)
    members = ensemble.shape[0]
    owned = ensemble.shape[1]
    cells = ensemble.shape[2]
    columns = lax.axis_size("member")
    regions = lax.axis_size("region")
    region_patches = owned * columns
    region = lax.axis_index("region")
    column = lax.axis_index("member")
    first = region * region_patches + column * owned
    links = lax.dynamic_slice_in_dim(neighbours, first, owned, 0)
    link_count = links.shape[1]
    widening = jnp.arange(link_count, dtype=jnp.float32) + 2.0
    home = (links // region_patches - region + 1) % regions
    within = links % region_patches
    position = home * region_patches + within
    position = position.reshape(-1)
    grid = jnp.arange(cells, dtype=jnp.int32)
    my_cells = lax.dynamic_slice_in_dim(obs_cell, first, owned, 0)
    my_values = lax.dynamic_slice_in_dim(obs_values, first, owned, 0)
    my_var = lax.dynamic_slice_in_dim(obs_var, first, owned, 0)
    flat_links = links.reshape(-1)
    for batch in range(NBATCH):
        picks = my_cells[:, batch, :]
        per_patch = picks.shape[1]
        selector = (picks[:, :, None] == grid[None, None, :]).astype(jnp.float32)
        own_rows = jnp.einsum("poc,kpc->pok", selector, ensemble, precision=HIGHEST)
        region_rows = collect(own_rows, "member", 0)
        beside_all = with_halo(region_rows, (("region", 0),), region_patches)
        far_rows = jnp.take(beside_all, position, axis=0).reshape(
            owned, link_count * per_patch, members
        )
        stacked = jnp.concatenate([own_rows, far_rows], axis=1)
        far_values = jnp.take(obs_values[:, batch, :], flat_links, axis=0).reshape(owned, -1)
        far_var = jnp.take(obs_var[:, batch, :], flat_links, axis=0).reshape(
            owned, link_count, per_patch
        )
        far_var = (far_var * widening[None, :, None]).reshape(owned, -1)
        wanted = jnp.concatenate([my_values[:, batch, :], far_values], axis=1)
        noise = jnp.concatenate([my_var[:, batch, :], far_var], axis=1)
        ensemble = jax.vmap(analyse, in_axes=(0, 0, 0, 1), out_axes=1)(
            stacked, wanted, noise, ensemble
        )
    return lax.all_to_all(ensemble, "member", split_axis=0, concat_axis=1, tiled=True)


def solution(mesh):
    in_specs = (P("member", "region", None), P(), P(), P(), P())
    out_specs = P("member", "region", None)
    return jax.shard_map(
        on_device, mesh=mesh, in_specs=in_specs, out_specs=out_specs, check_vma=False
    )
```

profile of v0, /device:TPU:1, one launch (start us, length us, event | category | flops | bytes accessed | tf_op | source)
XLA Modules:
  0.0 455.2 jit_solution(13198155324939116245)
XLA Ops:
  2.5 6.1 %all-to-all-start = ((f32[128,8,256]{2,0,1:T(8,128)}), f32[128,8,256]{2,0,1:T(8,128)S(1)}, u32[]{:S(2)}, u32[]{:S(2)}) async-start(f32[128,8,256]{2,0,1:T(8,128)} %copy.37), calls=%async_computation | async-start | bytes 2097152 | tf_op jit(solution)/shard_map/all_to_all | solution.py:59
  9.4 13.8 %all-to-all-done = f32[128,8,256]{2,0,1:T(8,128)S(1)} async-done(((f32[128,8,256]{2,0,1:T(8,128)}), f32[128,8,256]{2,0,1:T(8,128)S(1)}, u32[]{:S(2)}, u32[]{:S(2)}) %all-to-all-start) | async-done | bytes 1048608 | tf_op jit(solution)/shard_map/all_to_all | solution.py:59
  26.2 4.2 all-to-all-start.1
  31.0 24.9 %all-to-all-done.1 = f32[8,1,64,1024]{3,2,1,0:T(8,128)S(1)} async-done(((f32[8,1,64,1024]{3,2,1,0:T(8,128)}), f32[8,1,64,1024]{3,2,1,0:T(8,128)S(1)}, u32[]{:S(2)}, u32[]{:S(2)}) %all-to-all-start.1) | async-done | bytes 2097184 | tf_op jit(solution)/shard_map/all_to_all | solution.py:20
  55.9 4.8 %collective-permute-start = (f32[8,64,1024]{2,1,0:T(8,128)S(1)}, f32[8,64,1024]{2,1,0:T(8,128)}, u32[]{:S(2)}, u32[]{:S(2)}) collective-permute-start(f32[8,64,1024]{2,1,0:T(8,128)S(1)} %bitcast.334), channel_id=1, source_target_pairs={{0,8},{8,16},{16,24},{24,32},{32,40},{40,48},{48,56},{56,64},{64,7... | collective-permute-start | bytes 6291464 | tf_op jit(solution)/shard_map/ppermute | solution.py:34
  76.9 29.1 %collective-permute-done = f32[8,64,1024]{2,1,0:T(8,128)} collective-permute-done((f32[8,64,1024]{2,1,0:T(8,128)S(1)}, f32[8,64,1024]{2,1,0:T(8,128)}, u32[]{:S(2)}, u32[]{:S(2)}) %collective-permute-start) | collective-permute-done | bytes 2097184 | tf_op jit(solution)/shard_map/ppermute | solution.py:34
  106.1 3.5 collective-permute-done.1
  109.6 5.8 %pad_maximum_fusion = f32[24,64,1024]{2,1,0:T(8,128)} fusion(f32[8,64,1024]{2,1,0:T(8,128)} %collective-permute-done.1, f32[8,64,1024]{2,1,0:T(8,128)S(1)} %bitcast.336, f32[8,64,1024]{2,1,0:T(8,128)} %collective-permute-done), kind=kLoop, calls=%fused_computation.10 | loop fusion | flops 3145728 | bytes 12582912 | tf_op jit(solution)/shard_map/concatenate | solution.py:36
  115.4 4.5 gather_fusion.1
  128.2 11.7 %custom-call.28 = f32[1,128,128]{2,1,0:T(8,128)S(1)} custom-call(f32[1,128,128]{2,1,0:T(8,128)S(1)} %cholesky.308), custom_call_target="Cholesky" | custom-call | tf_op jit(solution)/shard_map/vmap(jit(cholesky))/cholesky | solution.py:51
  140.0 9.8 %custom-call.29 = f32[1,1,128,128]{2,3,1,0:T(8,128)S(1)} custom-call(f32[1,1,128,128]{3,2,1,0:T(8,128)S(1)} %get-tuple-element.70), custom_call_target="InvertDiagBlocksLowerTriangular" | custom-call | tf_op jit(solution)/shard_map/vmap(jit(cholesky))/cholesky | solution.py:51
  152.1 11.9 %custom-call.30 = f32[1,128,128]{2,1,0:T(8,128)S(1)} custom-call(f32[1,128,128]{2,1,0:T(8,128)S(1)} %cholesky.312), custom_call_target="Cholesky" | custom-call | tf_op jit(solution)/shard_map/vmap(jit(cholesky))/cholesky | solution.py:51
  165.4 9.8 %custom-call.31 = f32[1,1,128,128]{2,3,1,0:T(8,128)S(1)} custom-call(f32[1,1,128,128]{3,2,1,0:T(8,128)S(1)} %get-tuple-element.67), custom_call_target="InvertDiagBlocksLowerTriangular" | custom-call | tf_op jit(solution)/shard_map/vmap(jit(cholesky))/cholesky | solution.py:51
  176.5 11.7 %custom-call.32 = f32[1,128,128]{2,1,0:T(8,128)S(1)} custom-call(f32[1,128,128]{2,1,0:T(8,128)S(1)} %fusion.54), custom_call_target="Cholesky" | custom-call | tf_op jit(solution)/shard_map/vmap(jit(cholesky))/cholesky | solution.py:51
  192.7 6.2 %while.4 = (s32[]{:T(128)}, f32[1,384,384]{2,1,0:T(8,128)S(1)}, s32[3,2]{0,1:T(2,128)S(1)}, f32[3,1,128,128]{3,2,1,0:T(8,128)S(1)}, s32[]{:T(128)}) while((s32[]{:T(128)}, f32[1,384,384]{2,1,0:T(8,128)S(1)}, s32[3,2]{0,1:T(2,128)S(1)}, f32[3,1,128,128]{3,2,1,0:T(8,128)S(1)}, s32[]{:T(128)}) %tuple.62), condition=%wide.while_cond, body=%wide.while_body.sunk | while | flops 2 | bytes 131181 | solution.py:52
  199.0 30.1 %custom-call.33 = f32[1,3,128,128]{2,3,1,0:T(8,128)} custom-call(f32[1,3,128,128]{3,2,1,0:T(8,128)S(1)} %bitcast.363), custom_call_target="InvertDiagBlocksLowerTriangular" | custom-call | tf_op jit(solution)/shard_map/vmap(jit(_cho_solve))/triangular_solve | solution.py:52
  234.9 2.8 fusion.138
  238.7 19.4 %all_to_all.43 = f32[8,1,64,1024]{3,2,1,0:T(8,128)} all-to-all(f32[8,1,64,1024]{3,2,1,0:T(8,128)S(1)} %broadcast_in_dim.73), channel_id=1, replica_groups=mesh['region'=32,'member'=8] {'member'}, dimensions={0} | all-to-all | bytes 4194304 | tf_op jit(solution)/shard_map/all_to_all | solution.py:20
  258.1 22.2 %collective-permute-start.2 = (f32[8,64,1024]{2,1,0:T(8,128)}, f32[8,64,1024]{2,1,0:T(8,128)}, u32[]{:S(2)}, u32[]{:S(2)}) collective-permute-start(f32[8,64,1024]{2,1,0:T(8,128)} %bitcast.54), channel_id=1, source_target_pairs={{0,8},{8,16},{16,24},{24,32},{32,40},{40,48},{48,56},{56,64},{64,7... | collective-permute-start | bytes 6291464 | tf_op jit(solution)/shard_map/ppermute | solution.py:34
  280.8 23.8 %collective-permute-done.2 = f32[8,64,1024]{2,1,0:T(8,128)} collective-permute-done((f32[8,64,1024]{2,1,0:T(8,128)}, f32[8,64,1024]{2,1,0:T(8,128)}, u32[]{:S(2)}, u32[]{:S(2)}) %collective-permute-start.2) | collective-permute-done | bytes 2097184 | tf_op jit(solution)/shard_map/ppermute | solution.py:34
  304.6 3.2 collective-permute-done.3
  307.8 6.6 %pad_maximum_fusion.1 = f32[24,64,1024]{2,1,0:T(8,128)} fusion(f32[8,64,1024]{2,1,0:T(8,128)} %collective-permute-done.3, f32[8,64,1024]{2,1,0:T(8,128)} %bitcast.54, f32[8,64,1024]{2,1,0:T(8,128)} %collective-permute-done.2), kind=kLoop, calls=%fused_computation.11 | loop fusion | flops 3145728 | bytes 12582912 | tf_op jit(solution)/shard_map/concatenate | solution.py:36
  314.5 4.6 %gather_fusion.4 = f32[5,64,1024]{2,1,0:T(8,128)} fusion(f32[24,64,1024]{2,1,0:T(8,128)} %pad_maximum_fusion.1, s32[1024]{0:T(1024)} %copy-done.14), kind=kCustom, calls=%fused_computation.5.clone | custom fusion | bytes 2621460 | tf_op jit(solution)/shard_map/jit(_take)/gather | solution.py:88
  320.9 2.8 fusion.32
  326.7 11.7 %custom-call.34 = f32[1,128,128]{2,1,0:T(8,128)S(1)} custom-call(f32[1,128,128]{2,1,0:T(8,128)S(1)} %cholesky.316), custom_call_target="Cholesky" | custom-call | tf_op jit(solution)/shard_map/vmap(jit(cholesky))/cholesky | solution.py:51
  339.0 9.8 %custom-call.35 = f32[1,1,128,128]{2,3,1,0:T(8,128)S(1)} custom-call(f32[1,1,128,128]{3,2,1,0:T(8,128)S(1)} %get-tuple-element.63), custom_call_target="InvertDiagBlocksLowerTriangular" | custom-call | tf_op jit(solution)/shard_map/vmap(jit(cholesky))/cholesky | solution.py:51
  351.2 11.9 %custom-call.36 = f32[1,128,128]{2,1,0:T(8,128)S(1)} custom-call(f32[1,128,128]{2,1,0:T(8,128)S(1)} %cholesky.320), custom_call_target="Cholesky" | custom-call | tf_op jit(solution)/shard_map/vmap(jit(cholesky))/cholesky | solution.py:51
  365.2 9.8 %custom-call.37 = f32[1,1,128,128]{2,3,1,0:T(8,128)S(1)} custom-call(f32[1,1,128,128]{3,2,1,0:T(8,128)S(1)} %get-tuple-element.60), custom_call_target="InvertDiagBlocksLowerTriangular" | custom-call | tf_op jit(solution)/shard_map/vmap(jit(cholesky))/cholesky | solution.py:51
  376.3 11.7 %custom-call.38 = f32[1,128,128]{2,1,0:T(8,128)S(1)} custom-call(f32[1,128,128]{2,1,0:T(8,128)S(1)} %fusion.55), custom_call_target="Cholesky" | custom-call | tf_op jit(solution)/shard_map/vmap(jit(cholesky))/cholesky | solution.py:51
  391.8 6.6 %while.5 = (s32[]{:T(128)}, f32[1,384,384]{2,1,0:T(8,128)S(1)}, s32[3,2]{0,1:T(2,128)S(1)}, f32[3,1,128,128]{3,2,1,0:T(8,128)S(1)}, s32[]{:T(128)}) while((s32[]{:T(128)}, f32[1,384,384]{2,1,0:T(8,128)S(1)}, s32[3,2]{0,1:T(2,128)S(1)}, f32[3,1,128,128]{3,2,1,0:T(8,128)S(1)}, s32[]{:T(128)}) %tuple.68), condition=%wide.while_cond.clone, body=%wide.while_body.clone.sunk | while | flops 2 | bytes 131181 | solution.py:52
  399.1 30.3 %custom-call.39 = f32[1,3,128,128]{2,3,1,0:T(8,128)S(1)} custom-call(f32[1,3,128,128]{3,2,1,0:T(8,128)} %bitcast.362), custom_call_target="InvertDiagBlocksLowerTriangular" | custom-call | tf_op jit(solution)/shard_map/vmap(jit(_cho_solve))/triangular_solve | solution.py:52
  440.4 12.9 %all_to_all.44 = f32[1024,1,256]{2,1,0:T(1,128)S(1)} all-to-all(f32[1024,1,256]{2,1,0:T(1,128)S(1)} %copy.46), channel_id=1, replica_groups=mesh['region'=32,'member'=8] {'member'}, dimensions={0} | all-to-all | bytes 2097152 | tf_op jit(solution)/shard_map/all_to_all | solution.py:102
  (166 shorter events, 84.2 us)
Async XLA Ops:
  2.5 6.1 %copy-start.12 = (s32[256,2,64]{0,2,1:T(8,128)S(1)}, s32[256,2,64]{0,2,1:T(8,128)}, u32[]{:S(2)}) copy-start(s32[256,2,64]{0,2,1:T(8,128)} %param.14) | copy-start | bytes 393220
  2.5 20.6 %all-to-all-start = ((f32[128,8,256]{2,0,1:T(8,128)}), f32[128,8,256]{2,0,1:T(8,128)S(1)}, u32[]{:S(2)}, u32[]{:S(2)}) async-start(f32[128,8,256]{2,0,1:T(8,128)} %copy.37), calls=%async_computation | async-start | bytes 2097152 | tf_op jit(solution)/shard_map/all_to_all | solution.py:59
  23.8 0.7 copy-start
  26.2 4.2 copy-start.9
  26.2 34.6 %copy-start.10 = (f32[256,2,64]{0,2,1:T(8,128)S(1)}, f32[256,2,64]{0,2,1:T(8,128)}, u32[]{:S(2)}) copy-start(f32[256,2,64]{0,2,1:T(8,128)} %param.15) | copy-start | bytes 393220
  26.2 38.4 %copy-start.18 = (s32[256,5]{0,1:T(8,128)S(1)}, s32[256,5]{0,1:T(8,128)}, u32[]{:S(2)}) copy-start(s32[256,5]{0,1:T(8,128)} %param.13) | copy-start | bytes 15364
  26.2 29.7 %all-to-all-start.1 = ((f32[8,1,64,1024]{3,2,1,0:T(8,128)}), f32[8,1,64,1024]{3,2,1,0:T(8,128)S(1)}, u32[]{:S(2)}, u32[]{:S(2)}) async-start(f32[8,1,64,1024]{3,2,1,0:T(8,128)} %broadcast_in_dim.69), calls=%async_computation.1 | async-start | bytes 4194304 | tf_op jit(solution)/shard_map/all_to_all | solution.py:20
  55.9 50.2 %collective-permute-start = (f32[8,64,1024]{2,1,0:T(8,128)S(1)}, f32[8,64,1024]{2,1,0:T(8,128)}, u32[]{:S(2)}, u32[]{:S(2)}) collective-permute-start(f32[8,64,1024]{2,1,0:T(8,128)S(1)} %bitcast.334), channel_id=1, source_target_pairs={{0,8},{8,16},{16,24},{24,32},{32,40},{40,48},{48,56},{56,64},{64,7... | collective-permute-start | bytes 6291464 | tf_op jit(solution)/shard_map/ppermute | solution.py:34
  60.6 49.0 %collective-permute-start.1 = (f32[8,64,1024]{2,1,0:T(8,128)S(1)}, f32[8,64,1024]{2,1,0:T(8,128)}, u32[]{:S(2)}, u32[]{:S(2)}) collective-permute-start(f32[8,64,1024]{2,1,0:T(8,128)S(1)} %bitcast.335), channel_id=1, source_target_pairs={{8,0},{16,8},{24,16},{32,24},{40,32},{48,40},{56,48},{64,56},{72,6... | collective-permute-start | bytes 6291464 | tf_op jit(solution)/shard_map/ppermute | solution.py:35
  75.1 40.4 %copy-start.14 = (s32[1024]{0:T(1024)}, s32[1024]{0:T(1024)S(1)}, u32[]{:S(2)}) copy-start(s32[1024]{0:T(1024)S(1)} %pad_clamp_fusion) | copy-start | bytes 12292
  75.7 44.2 %copy-start.19 = (pred[5]{0:T(512)(128)(4,1)}, pred[5]{0:T(512)(128)(4,1)S(1)}, u32[]{:S(2)}) copy-start(pred[5]{0:T(512)(128)(4,1)S(1)} %compare_and_fusion) | copy-start | bytes 19
  119.9 1.6 copy-start.1
  127.3 0.8 copy-start.5
  188.3 2.7 copy-start.3
  229.1 2.7 copy-start.7
  232.7 2.2 copy-start.2
  232.7 2.2 copy-start.13
  234.9 2.9 copy-start.15
  238.7 42.0 %copy-start.17 = (f32[64]{0:T(128)S(1)}, f32[64]{0:T(128)}, u32[]{:S(2)}) copy-start(f32[64]{0:T(128)} %get-tuple-element.25) | copy-start | bytes 772
  258.1 46.4 %collective-permute-start.2 = (f32[8,64,1024]{2,1,0:T(8,128)}, f32[8,64,1024]{2,1,0:T(8,128)}, u32[]{:S(2)}, u32[]{:S(2)}) collective-permute-start(f32[8,64,1024]{2,1,0:T(8,128)} %bitcast.54), channel_id=1, source_target_pairs={{0,8},{8,16},{16,24},{24,32},{32,40},{40,48},{48,56},{56,64},{64,7... | collective-permute-start | bytes 6291464 | tf_op jit(solution)/shard_map/ppermute | solution.py:34
  280.4 27.4 %collective-permute-start.3 = (f32[8,64,1024]{2,1,0:T(8,128)}, f32[8,64,1024]{2,1,0:T(8,128)}, u32[]{:S(2)}, u32[]{:S(2)}) collective-permute-start(f32[8,64,1024]{2,1,0:T(8,128)} %bitcast.54), channel_id=1, source_target_pairs={{8,0},{16,8},{24,16},{32,24},{40,32},{48,40},{56,48},{64,56},{72,6... | collective-permute-start | bytes 6291464 | tf_op jit(solution)/shard_map/ppermute | solution.py:35
  314.5 4.6 %copy-start.20 = (pred[5]{0:T(512)(128)(4,1)S(1)}, pred[5]{0:T(512)(128)(4,1)}, u32[]{:S(2)}) copy-start(pred[5]{0:T(512)(128)(4,1)} %copy-done.19) | copy-start | bytes 19
  319.1 1.7 copy-start.16
  325.9 0.8 copy-start.6
  388.1 2.6 copy-start.4
  398.4 0.7 copy-start.11
  429.4 2.7 copy-start.8
where the time goes:
time: 460 us; the launch traced here: 455 us
  other arithmetic  201 us (44%)
  waiting for transfers between devices  98.3 us (21%)
  local copies, waits for them, and re-layouts  47.8 us (10%)
  starting transfers between devices  37.6 us (8%)
  matrix products  32.6 us (7%)
  blocking collectives  32.4 us (7%)
  between operations  4.66 us (1%)
    another operation x22, other arithmetic, analyse(): factor = jnp.linalg.cholesky(covariance)  115 us
    another operation x5, other arithmetic, analyse(): jax.scipy.linalg.cho_solve((factor, True), cross_cov) / (members - 1.0)  63.2 us
    ppermute x2, waiting for transfers between devices, with_halo(): before = lax.ppermute(last, axis, up)  52.9 us
    ppermute x2, starting transfers between devices, with_halo(): before = lax.ppermute(last, axis, up)  27 us
    all_to_all x1, waiting for transfers between devices, sent_to_all(): return lax.all_to_all(copies, axis, split_axis=0, concat_axis=0, tiled=True)  24.9 us
    all_to_all x1, blocking collectives, sent_to_all(): return lax.all_to_all(copies, axis, split_axis=0, concat_axis=0, tiled=True)  19.4 us
    all_to_all x1, waiting for transfers between devices, on_device(): lax.all_to_all(state, 'member', split_axis=1, concat_axis=0, tiled=True)  13.8 us
    all_to_all x1, blocking collectives, on_device(): lax.all_to_all(ensemble, 'member', split_axis=0, concat_axis=1, tiled=True)  12.9 us
  transfers between devices with their start and end apart: 6, of which 6 were waited for; matrix products, arithmetic and copies ran while one was open for 4% of the time, Pallas kernels for 0%

commit v1 on v0

v1 whole, which is shorter than its diff:
```python
import functools

import jax
import jax.numpy as jnp
from jax import lax
from jax.experimental import pallas as pl
from jax.experimental.pallas import tpu as pltpu
from jax.sharding import PartitionSpec as P

F32 = jnp.float32
BF16 = jnp.bfloat16
HIGHEST = lax.Precision.HIGHEST
MESH = pl.DeviceIdType.MESH
TILE = (8, 128)
OBS = 64
VMEM = pl.BlockSpec(memory_space=pltpu.VMEM)
SMEM = pl.BlockSpec(memory_space=pltpu.SMEM)


def dot(a, b, precision=None):
    return lax.dot_general(a, b, (((1,), (0,)), ((), ())), precision=precision, preferred_element_type=F32)


def dot_t(a, b, precision=None):
    return lax.dot_general(a, b, (((1,), (1,)), ((), ())), precision=precision, preferred_element_type=F32)


def split(x):
    high = x.astype(BF16)
    return high, (x - high.astype(F32)).astype(BF16)


def spread_tile(x):
    return jnp.broadcast_to(x, TILE)


def solve8(e, r):
    m = {}
    q = [None] * 8
    for i in range(0, 8, 2):
        a, b, d = e[i][i], e[i + 1][i], e[i + 1][i + 1]
        inv = 1.0 / (a * d - b * b)
        ai, bi, di = d * inv, b * inv, a * inv
        for k in range(i + 2, 8):
            m[k, i] = e[k][i] * ai - e[k][i + 1] * bi
            m[k, i + 1] = e[k][i + 1] * di - e[k][i] * bi
        for k in range(i + 2, 8):
            for j in range(i + 2, k + 1):
                e[k][j] = e[k][j] - (m[k, i] * e[j][i] + m[k, i + 1] * e[j][i + 1])
        for k in range(i + 2, 8):
            r[k] = r[k] - (m[k, i] * r[i] + m[k, i + 1] * r[i + 1])
        q[i], q[i + 1] = ai * r[i] - bi * r[i + 1], di * r[i + 1] - bi * r[i]
    for i in range(6, 0, -2):
        for k in range(i):
            q[k] = q[k] - (m[i, k] * q[i] + m[i + 1, k] * q[i + 1])
    return q


def inverse128(block):
    lane = lax.broadcasted_iota(jnp.int32, TILE, 1)
    sub = lax.broadcasted_iota(jnp.int32, TILE, 0)
    lanes = lax.broadcasted_iota(jnp.int32, (96, 128), 1)
    tiles = [block[8 * i : 8 * i + 8, :] for i in range(16)]
    for s in range(4):
        mine = list(range(4 * s, 4 * s + 4))
        others = [i for i in range(16) if i not in mine]
        old = jnp.concatenate([tiles[i] for i in others], axis=0)
        for t in mine:
            cols = {i: [spread_tile(tiles[i][:, 8 * t + k : 8 * t + k + 1]) for k in range(8)] for i in mine}
            e = [[spread_tile(cols[t][j][k : k + 1, :]) if j <= k else None for j in range(8)] for k in range(8)]
            inside = (lane >= 8 * t) & (lane < 8 * t + 8)
            rows = [
                jnp.where(lane == 8 * t + k, 1.0, jnp.where(inside, 0.0, spread_tile(tiles[t][k : k + 1, :])))
                for k in range(8)
            ]
            new = solve8(e, rows)
            for i in mine:
                if i == t:
                    u = new[0]
                    for k in range(1, 8):
                        u = jnp.where(sub == k, new[k], u)
                else:
                    u = jnp.where(inside, 0.0, tiles[i])
                    p = [cols[i][k] * new[k] for k in range(8)]
                    u = u - (((p[0] + p[1]) + (p[2] + p[3])) + ((p[4] + p[5]) + (p[6] + p[7])))
                tiles[i] = u
        low, high = 32 * s, 32 * s + 32
        parts = [jnp.concatenate([tiles[i] for i in mine], axis=0)]
        if low:
            parts.insert(0, jnp.zeros((low, 128), F32))
        if high < 128:
            parts.append(jnp.zeros((128 - high, 128), F32))
        strip = jnp.concatenate(parts, axis=0)
        inside = (lanes >= low) & (lanes < high)
        fresh = jnp.where(inside, 0.0, old) - dot(jnp.where(inside, old, 0.0), strip, HIGHEST)
        for q, i in enumerate(others):
            tiles[i] = fresh[8 * q : 8 * q + 8]
    return jnp.concatenate(tiles, axis=0)


def linked(nbr_ref, patch, home):
    first = last = first_at = last_at = jnp.int32(0)
    for j in range(5):
        n = nbr_ref[j, patch]
        here = (n >> 3) == home
        last = jnp.where(here, n, last)
        last_at = jnp.where(here, j, last_at)
    for j in reversed(range(5)):
        n = nbr_ref[j, patch]
        here = (n >> 3) == home
        first = jnp.where(here, n, first)
        first_at = jnp.where(here, j, first_at)
    return first, first_at, last, last_at


def place():
    region, member = lax.axis_index("region"), lax.axis_index("member")
    regions = lax.axis_size("region")
    sides = (region, lax.rem(region + 1, regions), lax.rem(region + regions - 1, regions))
    return region, member, sides


def columns(member):
    return pl.ds(pl.multiple_of(member * 128, 128), 128)


def greet(peers):
    barrier = pltpu.get_barrier_semaphore()
    for peer in peers:
        pl.semaphore_signal(barrier, inc=1, device_id=peer, device_id_type=MESH)
    pl.semaphore_wait(barrier, len(peers))


def all_peers(member, sides):
    return [
        {"region": sides[s], "member": lax.rem(member + d, 8)}
        for d in range(8)
        for s in range(3)
        if (s, d) != (0, 0)
    ]


def remote(src, dst, send, recv, region, member):
    return pltpu.make_async_remote_copy(
        src_ref=src,
        dst_ref=dst,
        send_sem=send,
        recv_sem=recv,
        device_id={"region": region, "member": member},
        device_id_type=MESH,
    )


def row_copies(own, region, member, sides, nbr_ref, rows, sbuf, y_ref, send_sem, recv_sem):
    low = 0 if own else OBS
    sent = []
    for d in range(8):
        other = lax.rem(member + d, 8)
        for s in (1, 2, 0):
            first, _, last, _ = linked(nbr_ref, sides[s] * 8 + other, region)
            if s == 0:
                if own:
                    sbuf[s, d, 0:OBS, :] = rows[other]
                sbuf[s, d, OBS : 2 * OBS, :] = rows[first & 7]
            else:
                sbuf[s, d, 0:OBS, :] = rows[first & 7]
                sbuf[s, d, OBS : 2 * OBS, :] = rows[last & 7]
            start = low if s == 0 else 0
            if s == 0 and d == 0:
                y_ref[start : 2 * OBS, columns(member)] = sbuf[0, 0, start : 2 * OBS, :]
                continue
            copy = remote(
                sbuf.at[s, d, pl.ds(start, 2 * OBS - start)],
                y_ref.at[pl.ds(s * 128 + start, 2 * OBS - start), columns(member)],
                send_sem.at[s, d],
                recv_sem.at[s, member],
                sides[s],
                other,
            )
            copy.start()
            sent.append(copy)
    return sent


def await_rows(own, member, sides, sbuf, y_ref, send_sem, recv_sem):
    low = 0 if own else OBS
    for d in range(8):
        other = lax.rem(member + d, 8)
        for s in range(3):
            if (s, d) == (0, 0):
                continue
            start = low if s == 0 else 0
            remote(
                sbuf.at[s, d, pl.ds(start, 2 * OBS - start)],
                y_ref.at[pl.ds(s * 128 + start, 2 * OBS - start), columns(other)],
                send_sem.at[s, d],
                recv_sem.at[s, other],
                sides[s],
                other,
            ).wait_recv()


def scatter_kernel(state_ref, cell_ref, nbr_ref, y_ref, x_ref, rows, sbuf, xbuf, send_sem, recv_sem, xsend_sem, xrecv_sem):
    region, member, sides = place()
    greet(all_peers(member, sides))
    lane = lax.broadcasted_iota(jnp.int32, (OBS, 256), 1)
    for q in range(8):
        cell = jnp.sum(jnp.where(lane == region * 8 + q, cell_ref[0], 0), axis=1, keepdims=True)
        picked = jnp.where(lane == cell, 1.0, 0.0)
        rows[q] = dot_t(picked, state_ref[:, q, :], HIGHEST)
    sent = row_copies(True, region, member, sides, nbr_ref, rows, sbuf, y_ref, send_sem, recv_sem)
    for q in range(8):
        xbuf[q] = state_ref[:, q, :].T
    for d in range(1, 8):
        other = lax.rem(member + d, 8)
        copy = remote(xbuf.at[other], x_ref.at[:, columns(member)], xsend_sem.at[d], xrecv_sem.at[member], region, other)
        copy.start()
        sent.append(copy)
    x_ref[:, columns(member)] = xbuf[member]
    await_rows(True, member, sides, sbuf, y_ref, send_sem, recv_sem)
    for d in range(1, 8):
        other = lax.rem(member + d, 8)
        remote(xbuf.at[other], x_ref.at[:, columns(other)], xsend_sem.at[d], xrecv_sem.at[other], region, other).wait_recv()
    for copy in sent:
        copy.wait_send()


def rows_kernel(own_ref, nbr_ref, y_ref, rows, sbuf, send_sem, recv_sem, asend_sem, arecv_sem):
    region, member, sides = place()
    greet(all_peers(member, sides))
    first = []
    for d in range(1, 8):
        other = lax.rem(member + d, 8)
        copy = remote(own_ref.at[:, columns(other)], rows.at[member], asend_sem.at[d], arecv_sem.at[member], region, other)
        copy.start()
        first.append(copy)
    rows[member] = own_ref[:, columns(member)]
    y_ref[0:OBS, :] = own_ref[...]
    for d in range(1, 8):
        other = lax.rem(member + d, 8)
        remote(own_ref.at[:, columns(other)], rows.at[other], asend_sem.at[d], arecv_sem.at[other], region, other).wait_recv()
    sent = row_copies(False, region, member, sides, nbr_ref, rows, sbuf, y_ref, send_sem, recv_sem)
    await_rows(False, member, sides, sbuf, y_ref, send_sem, recv_sem)
    for copy in first + sent:
        copy.wait_send()


def return_kernel(x_ref, o_ref, tbuf, send_sem, recv_sem):
    region, member, sides = place()
    greet([{"region": region, "member": lax.rem(member + d, 8)} for d in range(1, 8)])
    sent = []
    for d in range(1, 8):
        other = lax.rem(member + d, 8)
        tbuf[d] = x_ref[:, columns(other)].T
        copy = remote(tbuf.at[d], o_ref.at[member], send_sem.at[d], recv_sem.at[member], region, other)
        copy.start()
        sent.append(copy)
    o_ref[member] = x_ref[:, columns(member)].T
    for d in range(1, 8):
        other = lax.rem(member + d, 8)
        remote(tbuf.at[d], o_ref.at[other], send_sem.at[d], recv_sem.at[other], region, other).wait_recv()
    for copy in sent:
        copy.wait_send()


def analysis_kernel(batch, more, y_ref, x_ref, val_ref, var_ref, cell_ref, nbr_ref, *rest):
    if more:
        xo_ref, r_ref, yh, yl, ah, al, cov, inno, var, cross = rest
    else:
        xo_ref, yh, yl, ah, al, cov, inno, var, cross = rest
    region, member, sides = place()
    patch = region * 8 + member
    lane = lax.broadcasted_iota(jnp.int32, (OBS, 256), 1)
    same, same_at, _, _ = linked(nbr_ref, patch, region)
    slots = [(patch, jnp.int32(-1)), (same, same_at)]
    for side in (sides[2], sides[1]):
        f, fa, l, la = linked(nbr_ref, patch, side)
        slots += [(f, fa), (l, la)]
    for i, (n, at) in enumerate(slots):
        here = lane == n
        value = jnp.sum(jnp.where(here, val_ref[batch], 0.0), axis=1, keepdims=True)
        noise = jnp.sum(jnp.where(here, var_ref[batch], 0.0), axis=1, keepdims=True)
        widening = (at + 2).astype(F32)
        inno[i * OBS : (i + 1) * OBS, :] = jnp.broadcast_to(value, (OBS, 128))
        var[i * OBS : (i + 1) * OBS, :] = jnp.broadcast_to(noise * widening, (OBS, 128))

    def centre(i, _):
        at = pl.ds(pl.multiple_of(i * 32, 32), 32)
        y = y_ref[at, :]
        mean = jnp.sum(y, axis=1, keepdims=True) * (1.0 / 1024.0)
        yh[at, :], yl[at, :] = split(y - mean)
        inno[at, :] = inno[at, :] - mean
        return 0

    lax.fori_loop(0, 12, centre, 0)

    def covariance(i, _):
        at = pl.ds(pl.multiple_of(i * 128, 128), 128)
        high, low = yh[at, :], yl[at, :]
        total = dot_t(high, yh[...]) + (dot_t(high, yl[...]) + dot_t(low, yh[...]))
        row = lax.broadcasted_iota(jnp.int32, (128, 384), 0) + i * 128
        col = lax.broadcasted_iota(jnp.int32, (128, 384), 1)
        wide = jnp.concatenate([var[at, :]] * 3, axis=1)
        cov[at, :] = total * (1.0 / 1023.0) + jnp.where(row == col, wide, 0.0)
        return 0

    lax.fori_loop(0, 3, covariance, 0)

    def eliminate(k, _):
        at = pl.ds(pl.multiple_of(k * 128, 128), 128)
        inv = inverse128(cov[at, at])
        row = lax.broadcasted_iota(jnp.int32, (128, 384), 0) + k * 128
        col = lax.broadcasted_iota(jnp.int32, (128, 384), 1)
        inside = (col >= k * 128) & (col < k * 128 + 128)
        top = dot(inv, jnp.where(inside, jnp.where(row == col, 1.0, 0.0), cov[at, :]), HIGHEST)
        for i in range(3):
            part = slice(i * 128, i * 128 + 128)
            cov[part, :] = jnp.where(inside, 0.0, cov[part, :]) - dot(cov[part, at], top, HIGHEST)
        cov[at, :] = top
        return 0

    lax.fori_loop(0, 3, eliminate, 0)

    def anomaly(i, _):
        at = pl.ds(pl.multiple_of(i * 32, 32), 32)
        x = x_ref[at, :]
        ah[at, :], al[at, :] = split(x - jnp.sum(x, axis=1, keepdims=True) * (1.0 / 1024.0))
        return 0

    lax.fori_loop(0, 8, anomaly, 0)
    high, low = ah[...], al[...]
    cross[...] = (dot_t(high, yh[...]) + (dot_t(high, yl[...]) + dot_t(low, yh[...]))) * (1.0 / 1023.0)
    gain = dot(cross[...], cov[...], HIGHEST)
    shift = dot(gain, inno[...], HIGHEST)
    gh, gl = split(-0.5 * gain)
    if more:
        here = lane == patch
        cell = jnp.sum(jnp.where(here, cell_ref[batch + 1], 0), axis=1, keepdims=True)
        picked = jnp.where(lane == cell, 1.0, 0.0)
    for i in range(8):
        at = slice(i * 128, i * 128 + 128)
        h, l = yh[:, at], yl[:, at]
        x = x_ref[:, at] + (shift + (dot(gh, h) + (dot(gh, l) + dot(gl, h))))
        xo_ref[:, at] = x
        if more:
            r_ref[:, at] = dot(picked, x, HIGHEST)


def analysis(batch, more, y, x, values, variances, cells, nbr):
    out = [jax.ShapeDtypeStruct((256, 1024), F32)]
    if more:
        out.append(jax.ShapeDtypeStruct((OBS, 1024), F32))
    return pl.pallas_call(
        functools.partial(analysis_kernel, batch, more),
        out_shape=out,
        in_specs=[VMEM] * 5 + [SMEM],
        out_specs=[VMEM] * len(out),
        scratch_shapes=[
            pltpu.VMEM((384, 1024), BF16),
            pltpu.VMEM((384, 1024), BF16),
            pltpu.VMEM((256, 1024), BF16),
            pltpu.VMEM((256, 1024), BF16),
            pltpu.VMEM((384, 384), F32),
            pltpu.VMEM((384, 128), F32),
            pltpu.VMEM((384, 128), F32),
            pltpu.VMEM((256, 384), F32),
        ],
        compiler_params=pltpu.CompilerParams(vmem_limit_bytes=48 * 1024 * 1024),
        name="analysis",
    )(y, x, values, variances, cells, nbr)


DMA = pltpu.SemaphoreType.DMA


def params(number):
    return pltpu.CompilerParams(collective_id=number, has_side_effects=True, vmem_limit_bytes=48 * 1024 * 1024)


def on_device(state, neighbours, obs_cell, obs_values, obs_var):
    nbr = jnp.transpose(neighbours, (1, 0))
    cells = jnp.transpose(obs_cell, (1, 2, 0))
    values = jnp.transpose(obs_values, (1, 2, 0))
    variances = jnp.transpose(obs_var, (1, 2, 0))
    y, x = pl.pallas_call(
        scatter_kernel,
        out_shape=[jax.ShapeDtypeStruct((384, 1024), F32), jax.ShapeDtypeStruct((256, 1024), F32)],
        in_specs=[VMEM, VMEM, SMEM],
        out_specs=[VMEM, VMEM],
        scratch_shapes=[
            pltpu.VMEM((8, OBS, 128), F32),
            pltpu.VMEM((3, 8, 128, 128), F32),
            pltpu.VMEM((8, 256, 128), F32),
            DMA((3, 8)),
            DMA((3, 8)),
            DMA((8,)),
            DMA((8,)),
        ],
        compiler_params=params(0),
        name="scatter",
    )(state, cells, nbr)
    x, own = analysis(0, True, y, x, values, variances, cells, nbr)
    (y,) = pl.pallas_call(
        rows_kernel,
        out_shape=[jax.ShapeDtypeStruct((384, 1024), F32)],
        in_specs=[VMEM, SMEM],
        out_specs=[VMEM],
        scratch_shapes=[
            pltpu.VMEM((8, OBS, 128), F32),
            pltpu.VMEM((3, 8, 128, 128), F32),
            DMA((3, 8)),
            DMA((3, 8)),
            DMA((8,)),
            DMA((8,)),
        ],
        compiler_params=params(1),
        name="rows",
    )(own, nbr)
    (x,) = analysis(1, False, y, x, values, variances, cells, nbr)
    (out,) = pl.pallas_call(
        return_kernel,
        out_shape=[jax.ShapeDtypeStruct((8, 128, 256), F32)],
        in_specs=[VMEM],
        out_specs=[VMEM],
        scratch_shapes=[pltpu.VMEM((8, 128, 256), F32), DMA((8,)), DMA((8,))],
        compiler_params=params(2),
        name="give_back",
    )(x)
    return jnp.transpose(out, (1, 0, 2))


def solution(mesh):
    in_specs = (P("member", "region", None), P(), P(), P(), P())
    out_specs = P("member", "region", None)
    return jax.shard_map(on_device, mesh=mesh, in_specs=in_specs, out_specs=out_specs, check_vma=False)
```

time: 460 us -> 149 us (0.32)
  other arithmetic: 201 us -> 0 us
  Pallas kernels: 0 us -> 142 us
  waiting for transfers between devices: 98.3 us -> 0 us
  local copies, waits for them, and re-layouts: 47.8 us -> 6.23 us
  starting transfers between devices: 37.6 us -> 0 us
  matrix products: 32.6 us -> 0 us
  blocking collectives: 32.4 us -> 0 us
    another operation x27 -> x0, other arithmetic: 179 us -> none  [the longest x22 115 us: analyse(): factor = jnp.linalg.cholesky(covariance)]
    pallas_call x0 -> x5, Pallas kernels: none -> 142 us  [the longest x2 55 us: analysis(): pl.pallas_call(functools.partial(analysis_kernel, batch, more), out_shape...]
    ppermute x4 -> x0, waiting for transfers between devices: 59.7 us -> none  [the longest x2 52.9 us: with_halo(): before = lax.ppermute(last, axis, up)]
    all_to_all x2 -> x0, waiting for transfers between devices: 38.6 us -> none  [the longest x1 24.9 us: sent_to_all(): return lax.all_to_all(copies, axis, split_axis=0, concat_axis=0, tiled=True)]
    all_to_all x2 -> x0, blocking collectives: 32.4 us -> none  [the longest x1 19.4 us: sent_to_all(): return lax.all_to_all(copies, axis, split_axis=0, concat_axis=0, tiled=True)]
    ppermute x4 -> x0, starting transfers between devices: 27.3 us -> none  [the longest x2 27 us: with_halo(): before = lax.ppermute(last, axis, up)]
    dot_general x8 -> x0, matrix products: 16.9 us -> none  [the longest x2 5.69 us: analyse(): jnp.dot(spread, spread.T, precision=HIGHEST) / (members - 1.0)]
    another operation x28 -> x0, matrix products: 15.8 us -> none  [the longest x20 8.43 us: analyse(): jax.scipy.linalg.cho_solve((factor, True), cross_cov) / (members - 1.0)]
  transfers between devices with their start and end apart: 6 -> 0, of which waited for: 6 -> 0; matrix products, arithmetic and copies ran while one was open for 4% -> 0% of each run, Pallas kernels for 0% -> 0%
where the time goes in v1:
time: 149 us; the launch traced here: 148 us
  Pallas kernels  142 us (95%)
  local copies, waits for them, and re-layouts  6.23 us (4%)
    pallas_call x2, Pallas kernels, analysis(): pl.pallas_call(functools.partial(analysis_kernel, batch, more), out_shape...  55 us
    pallas_call x1, Pallas kernels, on_device(): pl.pallas_call(scatter_kernel, out_shape=[jax.ShapeDtypeStruct((384, 1024...  43 us
    pallas_call x1, Pallas kernels, on_device(): pl.pallas_call(rows_kernel, out_shape=[jax.ShapeDtypeStruct((384, 1024),...  26.2 us
    pallas_call x1, Pallas kernels, on_device(): pl.pallas_call(return_kernel, out_shape=[jax.ShapeDtypeStruct((8, 128, 25...  17.9 us
    unnamed x16, local copies, waits for them, and re-layouts  4.65 us

profile of v1, /device:TPU:1, one launch (start us, length us, event | category | flops | bytes accessed | tf_op | source)
XLA Modules:
  0.0 148.4 jit_solution(9788776893231596213)
XLA Ops:
  0.0 0.0 copy-start
  0.0 0.9 copy-done
  0.9 0.0 copy-start.2
  0.9 1.2 copy-done.2
  2.1 0.0 copy-start.7
  2.1 0.7 copy-done.7
  2.8 43.0 %scatter.1 = (f32[384,1024]{1,0:T(8,128)S(1)}, f32[256,1024]{1,0:T(8,128)S(1)}) custom-call(f32[128,8,256]{2,1,0:T(8,128)S(1)} %copy-done.2, s32[2,64,256]{2,1,0:T(8,128)S(1)} %bitcast.6, s32[5,256]{1,0:T(8,128)S(1)} %bitcast.13), custom_call_target="tpu_custom_call" | custom-call | tf_op jit(solution)/shard_map/scatter/pallas_call | solution.py:385
  45.8 0.0 copy-start.3
  45.8 0.9 copy-done.3
  46.7 0.0 copy-start.5
  46.7 0.9 copy-done.5
  47.6 28.3 %analysis.2 = (f32[256,1024]{1,0:T(8,128)S(1)}, f32[64,1024]{1,0:T(8,128)S(1)}) custom-call(f32[384,1024]{1,0:T(8,128)S(1)} %get-tuple-element.9.y_ref, f32[256,1024]{1,0:T(8,128)S(1)} %get-tuple-element.10.x_ref, f32[2,64,256]{2,1,0:T(8,128)S(1)} %bitcast.9, f32[2,64,256]{2,1,0:T(8,128)S(1)} %bitcast.11, s32[2,64,256]{2,1,0:T(8,128)S(1)} %bitcast.7, ...), custom_call_target="tpu_custom_call" | custom-call | tf_op jit(solution)/shard_map/analysis/pallas_call | solution.py:353
  75.9 0.0 copy-start.1
  76.0 0.0 copy-start.4
  76.0 0.0 copy-start.6
  76.0 26.2 %rows.1.y_ref = f32[384,1024]{1,0:T(8,128)S(1)} custom-call(f32[64,1024]{1,0:T(8,128)S(1)} %get-tuple-element.11.own_ref, s32[5,256]{1,0:T(8,128)S(1)} %bitcast.15), custom_call_target="tpu_custom_call" | custom-call | tf_op jit(solution)/shard_map/rows/pallas_call | solution.py:403
  102.2 0.0 copy-done.1
  102.2 0.0 copy-done.4
  102.2 0.0 copy-done.6
  102.3 26.7 %analysis.3.x_ref = f32[256,1024]{1,0:T(8,128)S(1)} custom-call(f32[384,1024]{1,0:T(8,128)S(1)} %rows.1.y_ref, f32[256,1024]{1,0:T(8,128)S(1)} %get-tuple-element.12.x_ref, f32[2,64,256]{2,1,0:T(8,128)S(1)} %bitcast.10, f32[2,64,256]{2,1,0:T(8,128)S(1)} %bitcast.12, s32[2,64,256]{2,1,0:T(8,128)S(1)} %bitcast.8, s32[5,256]{1,0:T(8,128)S(1)} %bitcast.16), custom_call_target="tpu_custom_call" | custom-call | tf_op jit(solution)/shard_map/analysis/pallas_call | solution.py:353
  128.9 17.9 %give_back.1 = f32[8,128,256]{2,1,0:T(8,128)S(1)} custom-call(f32[256,1024]{1,0:T(8,128)S(1)} %analysis.3.x_ref), custom_call_target="tpu_custom_call" | custom-call | tf_op jit(solution)/shard_map/give_back/pallas_call | solution.py:420
  146.8 1.6 %copy.6 = f32[128,8,256]{2,1,0:T(8,128)} copy(f32[128,8,256]{2,0,1:T(8,128)S(1)} %bitcast.5) | data formatting | bytes 2097152 | tf_op jit(solution)/shard_map/transpose | solution.py:429
Async XLA Ops:
  0.0 0.9 copy-start
  0.9 1.2 copy-start.2
  2.1 0.7 copy-start.7
  45.8 0.9 copy-start.3
  46.7 0.9 copy-start.5
  75.9 26.3 %copy-start.1 = (s32[256,2,64]{0,2,1:T(8,128)S(1)}, s32[256,2,64]{0,2,1:T(8,128)}, u32[]{:S(2)}) copy-start(s32[256,2,64]{0,2,1:T(8,128)} %param.7) | copy-start | bytes 393220
  76.0 26.3 %copy-start.4 = (f32[256,2,64]{0,2,1:T(8,128)S(1)}, f32[256,2,64]{0,2,1:T(8,128)}, u32[]{:S(2)}) copy-start(f32[256,2,64]{0,2,1:T(8,128)} %param.8) | copy-start | bytes 393220
  76.0 26.3 %copy-start.6 = (f32[256,2,64]{0,2,1:T(8,128)S(1)}, f32[256,2,64]{0,2,1:T(8,128)}, u32[]{:S(2)}) copy-start(f32[256,2,64]{0,2,1:T(8,128)} %param.9) | copy-start | bytes 393220

commit v2 on v1

v2 whole, which is shorter than its diff:
```python
import jax
import jax.numpy as jnp
from jax import lax
from jax.experimental import pallas as pl
from jax.experimental.pallas import tpu as pltpu
from jax.sharding import PartitionSpec as P

F32 = jnp.float32
BF16 = jnp.bfloat16
HIGHEST = lax.Precision.HIGHEST
MESH = pl.DeviceIdType.MESH
TILE = (8, 128)
OBS = 64
VMEM = pl.BlockSpec(memory_space=pltpu.VMEM)
SMEM = pl.BlockSpec(memory_space=pltpu.SMEM)
ANY = pl.BlockSpec(memory_space=pl.ANY)
DMA = pltpu.SemaphoreType.DMA


def dot(a, b, precision=None):
    return lax.dot_general(a, b, (((1,), (0,)), ((), ())), precision=precision, preferred_element_type=F32)


def dot_t(a, b, precision=None):
    return lax.dot_general(a, b, (((1,), (1,)), ((), ())), precision=precision, preferred_element_type=F32)


def split(x):
    high = x.astype(BF16)
    return high, (x - high.astype(F32)).astype(BF16)


def spread_tile(x):
    return jnp.broadcast_to(x, TILE)


def solve8(e, r):
    m = {}
    q = [None] * 8
    for i in range(0, 8, 2):
        a, b, d = e[i][i], e[i + 1][i], e[i + 1][i + 1]
        inv = 1.0 / (a * d - b * b)
        ai, bi, di = d * inv, b * inv, a * inv
        for k in range(i + 2, 8):
            m[k, i] = e[k][i] * ai - e[k][i + 1] * bi
            m[k, i + 1] = e[k][i + 1] * di - e[k][i] * bi
        for k in range(i + 2, 8):
            for j in range(i + 2, k + 1):
                e[k][j] = e[k][j] - (m[k, i] * e[j][i] + m[k, i + 1] * e[j][i + 1])
        for k in range(i + 2, 8):
            r[k] = r[k] - (m[k, i] * r[i] + m[k, i + 1] * r[i + 1])
        q[i], q[i + 1] = ai * r[i] - bi * r[i + 1], di * r[i + 1] - bi * r[i]
    for i in range(6, 0, -2):
        for k in range(i):
            q[k] = q[k] - (m[i, k] * q[i] + m[i + 1, k] * q[i + 1])
    return q


def inverse128(block):
    lane = lax.broadcasted_iota(jnp.int32, TILE, 1)
    sub = lax.broadcasted_iota(jnp.int32, TILE, 0)
    lanes = lax.broadcasted_iota(jnp.int32, (96, 128), 1)
    tiles = [block[8 * i : 8 * i + 8, :] for i in range(16)]
    for s in range(4):
        mine = list(range(4 * s, 4 * s + 4))
        others = [i for i in range(16) if i not in mine]
        old = jnp.concatenate([tiles[i] for i in others], axis=0)
        for t in mine:
            cols = {i: [spread_tile(tiles[i][:, 8 * t + k : 8 * t + k + 1]) for k in range(8)] for i in mine}
            e = [[spread_tile(cols[t][j][k : k + 1, :]) if j <= k else None for j in range(8)] for k in range(8)]
            inside = (lane >= 8 * t) & (lane < 8 * t + 8)
            rows = [
                jnp.where(lane == 8 * t + k, 1.0, jnp.where(inside, 0.0, spread_tile(tiles[t][k : k + 1, :])))
                for k in range(8)
            ]
            new = solve8(e, rows)
            for i in mine:
                if i == t:
                    u = new[0]
                    for k in range(1, 8):
                        u = jnp.where(sub == k, new[k], u)
                else:
                    u = jnp.where(inside, 0.0, tiles[i])
                    p = [cols[i][k] * new[k] for k in range(8)]
                    u = u - (((p[0] + p[1]) + (p[2] + p[3])) + ((p[4] + p[5]) + (p[6] + p[7])))
                tiles[i] = u
        low, high = 32 * s, 32 * s + 32
        parts = [jnp.concatenate([tiles[i] for i in mine], axis=0)]
        if low:
            parts.insert(0, jnp.zeros((low, 128), F32))
        if high < 128:
            parts.append(jnp.zeros((128 - high, 128), F32))
        strip = jnp.concatenate(parts, axis=0)
        inside = (lanes >= low) & (lanes < high)
        fresh = jnp.where(inside, 0.0, old) - dot(jnp.where(inside, old, 0.0), strip, HIGHEST)
        for q, i in enumerate(others):
            tiles[i] = fresh[8 * q : 8 * q + 8]
    return jnp.concatenate(tiles, axis=0)


def linked(nbr_ref, patch, home):
    first = last = first_at = last_at = jnp.int32(0)
    for j in range(5):
        n = nbr_ref[j, patch]
        here = (n >> 3) == home
        last = jnp.where(here, n, last)
        last_at = jnp.where(here, j, last_at)
    for j in reversed(range(5)):
        n = nbr_ref[j, patch]
        here = (n >> 3) == home
        first = jnp.where(here, n, first)
        first_at = jnp.where(here, j, first_at)
    return first, first_at, last, last_at


def place():
    region, member = lax.axis_index("region"), lax.axis_index("member")
    regions = lax.axis_size("region")
    sides = (region, lax.rem(region + 1, regions), lax.rem(region + regions - 1, regions))
    return region, member, sides


def columns(member):
    return pl.ds(pl.multiple_of(member * 128, 128), 128)


def all_peers(member, sides):
    return [
        {"region": sides[s], "member": lax.rem(member + d, 8)}
        for d in range(8)
        for s in range(3)
        if (s, d) != (0, 0)
    ]


def remote(src, dst, send, recv, region, member):
    return pltpu.make_async_remote_copy(
        src_ref=src,
        dst_ref=dst,
        send_sem=send,
        recv_sem=recv,
        device_id={"region": region, "member": member},
        device_id_type=MESH,
    )


def exchange(batch, region, member, sides, nbr_ref, rows, sbuf, y_ref, send_sem, recv_sem):
    low = OBS if batch else 0
    sent = []
    for d in range(8):
        other = lax.rem(member + d, 8)
        for s in (1, 2, 0):
            first, _, last, _ = linked(nbr_ref, sides[s] * 8 + other, region)
            if s == 0:
                if batch == 0:
                    sbuf[batch, s, d, 0:OBS, :] = rows[batch, other]
                sbuf[batch, s, d, OBS : 2 * OBS, :] = rows[batch, first & 7]
            else:
                sbuf[batch, s, d, 0:OBS, :] = rows[batch, first & 7]
                sbuf[batch, s, d, OBS : 2 * OBS, :] = rows[batch, last & 7]
            start = low if s == 0 else 0
            if s == 0 and d == 0:
                y_ref[batch, start : 2 * OBS, columns(member)] = sbuf[batch, 0, 0, start : 2 * OBS, :]
                continue
            copy = remote(
                sbuf.at[batch, s, d, pl.ds(start, 2 * OBS - start)],
                y_ref.at[batch, pl.ds(s * 128 + start, 2 * OBS - start), columns(member)],
                send_sem.at[batch, s, d],
                recv_sem.at[batch, s, member],
                sides[s],
                other,
            )
            copy.start()
            sent.append(copy)
    return sent


def await_rows(batch, member, sides, sbuf, y_ref, send_sem, recv_sem):
    low = OBS if batch else 0
    for d in range(8):
        other = lax.rem(member + d, 8)
        for s in range(3):
            if (s, d) == (0, 0):
                continue
            start = low if s == 0 else 0
            remote(
                sbuf.at[batch, s, d, pl.ds(start, 2 * OBS - start)],
                y_ref.at[batch, pl.ds(s * 128 + start, 2 * OBS - start), columns(other)],
                send_sem.at[batch, s, d],
                recv_sem.at[batch, s, other],
                sides[s],
                other,
            ).wait_recv()


def observed(batch, patch, region, sides, nbr_ref, val_ref, var_ref, inno, var):
    lane = lax.broadcasted_iota(jnp.int32, (OBS, 256), 1)
    same, same_at, _, _ = linked(nbr_ref, patch, region)
    slots = [(patch, jnp.int32(-1)), (same, same_at)]
    for side in (sides[2], sides[1]):
        f, fa, l, la = linked(nbr_ref, patch, side)
        slots += [(f, fa), (l, la)]
    for i, (n, at) in enumerate(slots):
        here = lane == n
        value = jnp.sum(jnp.where(here, val_ref[batch], 0.0), axis=1, keepdims=True)
        noise = jnp.sum(jnp.where(here, var_ref[batch], 0.0), axis=1, keepdims=True)
        widening = (at + 2).astype(F32)
        inno[i * OBS : (i + 1) * OBS, :] = jnp.broadcast_to(value, (OBS, 128))
        var[i * OBS : (i + 1) * OBS, :] = jnp.broadcast_to(noise * widening, (OBS, 128))


def inverse_covariance(batch, y_ref, yh, yl, cov, inno, var):
    def centre(i, _):
        at = pl.ds(pl.multiple_of(i * 32, 32), 32)
        y = y_ref[batch, at, :]
        mean = jnp.sum(y, axis=1, keepdims=True) * (1.0 / 1024.0)
        yh[at, :], yl[at, :] = split(y - mean)
        inno[at, :] = inno[at, :] - mean
        return 0

    lax.fori_loop(0, 12, centre, 0)

    def covariance(i, _):
        at = pl.ds(pl.multiple_of(i * 128, 128), 128)
        high, low = yh[at, :], yl[at, :]
        total = dot_t(high, yh[...]) + (dot_t(high, yl[...]) + dot_t(low, yh[...]))
        row = lax.broadcasted_iota(jnp.int32, (128, 384), 0) + i * 128
        col = lax.broadcasted_iota(jnp.int32, (128, 384), 1)
        wide = jnp.concatenate([var[at, :]] * 3, axis=1)
        cov[at, :] = total * (1.0 / 1023.0) + jnp.where(row == col, wide, 0.0)
        return 0

    lax.fori_loop(0, 3, covariance, 0)

    def eliminate(k, _):
        at = pl.ds(pl.multiple_of(k * 128, 128), 128)
        inv = inverse128(cov[at, at])
        row = lax.broadcasted_iota(jnp.int32, (128, 384), 0) + k * 128
        col = lax.broadcasted_iota(jnp.int32, (128, 384), 1)
        inside = (col >= k * 128) & (col < k * 128 + 128)
        top = dot(inv, jnp.where(inside, jnp.where(row == col, 1.0, 0.0), cov[at, :]), HIGHEST)
        for i in range(3):
            part = slice(i * 128, i * 128 + 128)
            cov[part, :] = jnp.where(inside, 0.0, cov[part, :]) - dot(cov[part, at], top, HIGHEST)
        cov[at, :] = top
        return 0

    lax.fori_loop(0, 3, eliminate, 0)


def gain_of(x_ref, yh, yl, ah, al, cov, inno):
    def anomaly(i, _):
        at = pl.ds(pl.multiple_of(i * 32, 32), 32)
        x = x_ref[at, :]
        ah[at, :], al[at, :] = split(x - jnp.sum(x, axis=1, keepdims=True) * (1.0 / 1024.0))
        return 0

    lax.fori_loop(0, 8, anomaly, 0)
    high, low = ah[...], al[...]
    cross = (dot_t(high, yh[...]) + (dot_t(high, yl[...]) + dot_t(low, yh[...]))) * (1.0 / 1023.0)
    gain = dot(cross, cov[...], HIGHEST)
    return gain, dot(gain, inno[...], HIGHEST)


def whole_kernel(
    state_hbm, cell_hbm, val_hbm, var_hbm, nbr_ref, o_ref,
    state_ref, cell_ref, val_ref, var_ref,
    rows, sbuf, y_ref, xbuf, x_ref, x2_ref, rbuf, tbuf,
    yh, yl, ah, al, cov, inno, var,
    load_sem, send_sem, recv_sem, xsend_sem, xrecv_sem, asend_sem, arecv_sem, osend_sem, orecv_sem,
):
    region, member, sides = place()
    patch = region * 8 + member
    lane = lax.broadcasted_iota(jnp.int32, (OBS, 256), 1)
    loads = [
        pltpu.make_async_copy(src, dst, load_sem.at[i])
        for i, (src, dst) in enumerate(
            ((state_hbm, state_ref), (cell_hbm, cell_ref), (val_hbm, val_ref), (var_hbm, var_ref))
        )
    ]
    for load in loads:
        load.start()
    peers = all_peers(member, sides)
    barrier = pltpu.get_barrier_semaphore()
    for peer in peers:
        pl.semaphore_signal(barrier, inc=1, device_id=peer, device_id_type=MESH)
    loads[0].wait()
    loads[1].wait()
    for q in range(8):
        cell = jnp.sum(jnp.where(lane == region * 8 + q, cell_ref[0], 0), axis=1, keepdims=True)
        picked = jnp.where(lane == cell, 1.0, 0.0)
        rows[0, q] = dot_t(picked, state_ref[:, q, :], HIGHEST)
    pl.semaphore_wait(barrier, len(peers))

    sent = exchange(0, region, member, sides, nbr_ref, rows, sbuf, y_ref, send_sem, recv_sem)
    for q in range(8):
        xbuf[q] = state_ref[:, q, :].T
    x_ref[:, columns(member)] = xbuf[member]
    loads[2].wait()
    loads[3].wait()
    observed(0, patch, region, sides, nbr_ref, val_ref, var_ref, inno, var)
    await_rows(0, member, sides, sbuf, y_ref, send_sem, recv_sem)
    for d in range(1, 8):
        other = lax.rem(member + d, 8)
        copy = remote(xbuf.at[other], x_ref.at[:, columns(member)], xsend_sem.at[d], xrecv_sem.at[member], region, other)
        copy.start()
        sent.append(copy)
    inverse_covariance(0, y_ref, yh, yl, cov, inno, var)
    for d in range(1, 8):
        other = lax.rem(member + d, 8)
        remote(xbuf.at[other], x_ref.at[:, columns(other)], xsend_sem.at[d], xrecv_sem.at[other], region, other).wait_recv()

    gain, shift = gain_of(x_ref, yh, yl, ah, al, cov, inno)
    cell = jnp.sum(jnp.where(lane == patch, cell_ref[1], 0), axis=1, keepdims=True)
    picked = jnp.where(lane == cell, 1.0, 0.0)
    pshift = dot(picked, shift, HIGHEST)
    ph, pl_ = split(dot(picked, -0.5 * gain, HIGHEST))
    for d in range(8):
        other = lax.rem(member + d, 8)
        at = columns(other)
        h, l = yh[:, at], yl[:, at]
        r = dot(picked, x_ref[:, at], HIGHEST) + (pshift + (dot(ph, h) + (dot(ph, l) + dot(pl_, h))))
        rbuf[d] = r
        y_ref[1, 0:OBS, at] = r
        if d == 0:
            rows[1, member] = r
            continue
        copy = remote(rbuf.at[d], rows.at[1, member], asend_sem.at[d], arecv_sem.at[member], region, other)
        copy.start()
        sent.append(copy)
    gh, gl = split(-0.5 * gain)
    for i in range(8):
        at = slice(i * 128, i * 128 + 128)
        h, l = yh[:, at], yl[:, at]
        x2_ref[:, at] = x_ref[:, at] + (shift + (dot(gh, h) + (dot(gh, l) + dot(gl, h))))
    for d in range(1, 8):
        other = lax.rem(member + d, 8)
        remote(rbuf.at[d], rows.at[1, other], asend_sem.at[d], arecv_sem.at[other], region, other).wait_recv()

    sent += exchange(1, region, member, sides, nbr_ref, rows, sbuf, y_ref, send_sem, recv_sem)
    observed(1, patch, region, sides, nbr_ref, val_ref, var_ref, inno, var)
    await_rows(1, member, sides, sbuf, y_ref, send_sem, recv_sem)
    inverse_covariance(1, y_ref, yh, yl, cov, inno, var)
    gain, shift = gain_of(x2_ref, yh, yl, ah, al, cov, inno)
    gh, gl = split(-0.5 * gain)
    for d in (1, 2, 3, 4, 5, 6, 7, 0):
        other = lax.rem(member + d, 8)
        at = columns(other)
        h, l = yh[:, at], yl[:, at]
        x = x2_ref[:, at] + (shift + (dot(gh, h) + (dot(gh, l) + dot(gl, h))))
        if d == 0:
            o_ref[member] = x.T
            continue
        tbuf[d] = x.T
        copy = remote(tbuf.at[d], o_ref.at[member], osend_sem.at[d], orecv_sem.at[member], region, other)
        copy.start()
        sent.append(copy)
    for d in range(1, 8):
        other = lax.rem(member + d, 8)
        remote(tbuf.at[d], o_ref.at[other], osend_sem.at[d], orecv_sem.at[other], region, other).wait_recv()
    for copy in sent:
        copy.wait_send()


def on_device(state, neighbours, obs_cell, obs_values, obs_var):
    small = pltpu.VMEM((2, OBS, 256), F32)
    out = pl.pallas_call(
        whole_kernel,
        out_shape=jax.ShapeDtypeStruct((8, 128, 256), F32),
        in_specs=[ANY] * 4 + [SMEM],
        out_specs=VMEM,
        scratch_shapes=[
            pltpu.VMEM((128, 8, 256), F32),
            pltpu.VMEM((2, OBS, 256), jnp.int32),
            small,
            small,
            pltpu.VMEM((2, 8, OBS, 128), F32),
            pltpu.VMEM((2, 3, 8, 128, 128), F32),
            pltpu.VMEM((2, 384, 1024), F32),
            pltpu.VMEM((8, 256, 128), F32),
            pltpu.VMEM((256, 1024), F32),
            pltpu.VMEM((256, 1024), F32),
            pltpu.VMEM((8, OBS, 128), F32),
            pltpu.VMEM((8, 128, 256), F32),
            pltpu.VMEM((384, 1024), BF16),
            pltpu.VMEM((384, 1024), BF16),
            pltpu.VMEM((256, 1024), BF16),
            pltpu.VMEM((256, 1024), BF16),
            pltpu.VMEM((384, 384), F32),
            pltpu.VMEM((384, 128), F32),
            pltpu.VMEM((384, 128), F32),
            DMA((4,)),
            DMA((2, 3, 8)),
            DMA((2, 3, 8)),
            DMA((8,)),
            DMA((8,)),
            DMA((8,)),
            DMA((8,)),
            DMA((8,)),
            DMA((8,)),
        ],
        compiler_params=pltpu.CompilerParams(
            collective_id=0, has_side_effects=True, vmem_limit_bytes=60 * 1024 * 1024
        ),
        name="whole",
    )(
        state,
        jnp.transpose(obs_cell, (1, 2, 0)),
        jnp.transpose(obs_values, (1, 2, 0)),
        jnp.transpose(obs_var, (1, 2, 0)),
        jnp.transpose(neighbours, (1, 0)),
    )
    return jnp.transpose(out, (1, 0, 2))


def solution(mesh):
    in_specs = (P("member", "region", None), P(), P(), P(), P())
    out_specs = P("member", "region", None)
    return jax.shard_map(on_device, mesh=mesh, in_specs=in_specs, out_specs=out_specs, check_vma=False)
```

time: 149 us -> 123 us (0.83)
  Pallas kernels: 142 us -> 120 us
  local copies, waits for them, and re-layouts: 6.23 us -> 2.81 us
    pallas_call x5 -> x1, Pallas kernels: 142 us -> 120 us  [on_device(): pl.pallas_call(whole_kernel, out_shape=jax.ShapeDtypeStruct((8, 128, 256)...]
    unnamed x16 -> x0, local copies, waits for them, and re-layouts: 4.65 us -> none
where the time goes in v2:
time: 123 us; the launch traced here: 122 us
  Pallas kernels  120 us (98%)
  local copies, waits for them, and re-layouts  2.81 us (2%)
    pallas_call x1, Pallas kernels, on_device(): pl.pallas_call(whole_kernel, out_shape=jax.ShapeDtypeStruct((8, 128, 256)...  120 us
    transpose x1, local copies, waits for them, and re-layouts, on_device(): return jnp.transpose(out, (1, 0, 2))  2.81 us

profile of v2, /device:TPU:1, one launch (start us, length us, event | category | flops | bytes accessed | tf_op | source)
XLA Modules:
  0.0 122.4 jit_solution(12949885365785059402)
XLA Ops:
  0.0 119.6 %whole.1 = f32[8,128,256]{2,1,0:T(8,128)} custom-call(f32[128,8,256]{2,1,0:T(8,128)} %state_hbm.1, s32[2,64,256]{2,1,0:T(8,128)} %bitcast.6, f32[2,64,256]{2,1,0:T(8,128)} %bitcast.7, f32[2,64,256]{2,1,0:T(8,128)} %bitcast.8, s32[5,256]{1,0:T(8,128)} %bitcast.9), custom_call_target="tpu_custom_call" | custom-call | tf_op jit(solution)/shard_map/whole/pallas_call | solution.py:367
  119.6 2.8 %copy.6 = f32[128,8,256]{2,1,0:T(8,128)} copy(f32[128,8,256]{2,0,1:T(8,128)} %bitcast.5) | data formatting | bytes 2097152 | tf_op jit(solution)/shard_map/transpose | solution.py:413

commit v3 on v2

--- a/solution.py
+++ b/solution.py
@@ -59,14 +59,13 @@
 def inverse128(block):
     lane = lax.broadcasted_iota(jnp.int32, TILE, 1)
     sub = lax.broadcasted_iota(jnp.int32, TILE, 0)
-    lanes = lax.broadcasted_iota(jnp.int32, (96, 128), 1)
-    tiles = [block[8 * i : 8 * i + 8, :] for i in range(16)]
-    for s in range(4):
-        mine = list(range(4 * s, 4 * s + 4))
-        others = [i for i in range(16) if i not in mine]
-        old = jnp.concatenate([tiles[i] for i in others], axis=0)
-        for t in mine:
-            cols = {i: [spread_tile(tiles[i][:, 8 * t + k : 8 * t + k + 1]) for k in range(8)] for i in mine}
+    front = lax.broadcasted_iota(jnp.int32, (96, 128), 1) < 32
+
+    def strip(_, matrix):
+        tiles = [matrix[8 * i : 8 * i + 8, :] for i in range(4)]
+        old = matrix[32:, :]
+        for t in range(4):
+            cols = [[spread_tile(tile[:, 8 * t + k : 8 * t + k + 1]) for k in range(8)] for tile in tiles]
             e = [[spread_tile(cols[t][j][k : k + 1, :]) if j <= k else None for j in range(8)] for k in range(8)]
             inside = (lane >= 8 * t) & (lane < 8 * t + 8)
             rows = [
@@ -74,28 +73,22 @@
                 for k in range(8)
             ]
             new = solve8(e, rows)
-            for i in mine:
+            for i in range(4):
                 if i == t:
                     u = new[0]
                     for k in range(1, 8):
                         u = jnp.where(sub == k, new[k], u)
                 else:
+                    p = [cols[i][k] * new[k] for k in range(8)]
                     u = jnp.where(inside, 0.0, tiles[i])
-                    p = [cols[i][k] * new[k] for k in range(8)]
                     u = u - (((p[0] + p[1]) + (p[2] + p[3])) + ((p[4] + p[5]) + (p[6] + p[7])))
                 tiles[i] = u
-        low, high = 32 * s, 32 * s + 32
-        parts = [jnp.concatenate([tiles[i] for i in mine], axis=0)]
-        if low:
-            parts.insert(0, jnp.zeros((low, 128), F32))
-        if high < 128:
-            parts.append(jnp.zeros((128 - high, 128), F32))
-        strip = jnp.concatenate(parts, axis=0)
-        inside = (lanes >= low) & (lanes < high)
-        fresh = jnp.where(inside, 0.0, old) - dot(jnp.where(inside, old, 0.0), strip, HIGHEST)
-        for q, i in enumerate(others):
-            tiles[i] = fresh[8 * q : 8 * q + 8]
-    return jnp.concatenate(tiles, axis=0)
+        top = jnp.concatenate(tiles, axis=0)
+        padded = jnp.concatenate([top, jnp.zeros((96, 128), F32)], axis=0)
+        fresh = jnp.where(front, 0.0, old) - dot(jnp.where(front, old, 0.0), padded, HIGHEST)
+        return pltpu.roll(jnp.concatenate([fresh, top], axis=0), 96, 1)
+
+    return lax.fori_loop(0, 4, strip, block)
 
 
 def linked(nbr_ref, patch, home):
@@ -144,12 +137,16 @@
     )
 
 
+def start_of(batch, s):
+    return OBS if batch and s == 0 else 0
+
+
 def exchange(batch, region, member, sides, nbr_ref, rows, sbuf, y_ref, send_sem, recv_sem):
-    low = OBS if batch else 0
     sent = []
-    for d in range(8):
-        other = lax.rem(member + d, 8)
-        for s in (1, 2, 0):
+    for s in range(3):
+        start = start_of(batch, s)
+        for d in range(8):
+            other = lax.rem(member + d, 8)
             first, _, last, _ = linked(nbr_ref, sides[s] * 8 + other, region)
             if s == 0:
                 if batch == 0:
@@ -158,7 +155,6 @@
             else:
                 sbuf[batch, s, d, 0:OBS, :] = rows[batch, first & 7]
                 sbuf[batch, s, d, OBS : 2 * OBS, :] = rows[batch, last & 7]
-            start = low if s == 0 else 0
             if s == 0 and d == 0:
                 y_ref[batch, start : 2 * OBS, columns(member)] = sbuf[batch, 0, 0, start : 2 * OBS, :]
                 continue
@@ -175,22 +171,20 @@
     return sent
 
 
-def await_rows(batch, member, sides, sbuf, y_ref, send_sem, recv_sem):
-    low = OBS if batch else 0
+def await_side(batch, s, member, sides, sbuf, y_ref, send_sem, recv_sem):
+    start = start_of(batch, s)
     for d in range(8):
-        other = lax.rem(member + d, 8)
-        for s in range(3):
-            if (s, d) == (0, 0):
-                continue
-            start = low if s == 0 else 0
-            remote(
-                sbuf.at[batch, s, d, pl.ds(start, 2 * OBS - start)],
-                y_ref.at[batch, pl.ds(s * 128 + start, 2 * OBS - start), columns(other)],
-                send_sem.at[batch, s, d],
-                recv_sem.at[batch, s, other],
-                sides[s],
-                other,
-            ).wait_recv()
+        if (s, d) == (0, 0):
+            continue
+        other = lax.rem(member + d, 8)
+        remote(
+            sbuf.at[batch, s, d, pl.ds(start, 2 * OBS - start)],
+            y_ref.at[batch, pl.ds(s * 128 + start, 2 * OBS - start), columns(other)],
+            send_sem.at[batch, s, d],
+            recv_sem.at[batch, s, other],
+            sides[s],
+            other,
+        ).wait_recv()
 
 
 def observed(batch, patch, region, sides, nbr_ref, val_ref, var_ref, inno, var):
@@ -209,46 +203,63 @@
         var[i * OBS : (i + 1) * OBS, :] = jnp.broadcast_to(noise * widening, (OBS, 128))
 
 
-def inverse_covariance(batch, y_ref, yh, yl, cov, inno, var):
-    def centre(i, _):
-        at = pl.ds(pl.multiple_of(i * 32, 32), 32)
-        y = y_ref[batch, at, :]
-        mean = jnp.sum(y, axis=1, keepdims=True) * (1.0 / 1024.0)
-        yh[at, :], yl[at, :] = split(y - mean)
-        inno[at, :] = inno[at, :] - mean
-        return 0
-
-    lax.fori_loop(0, 12, centre, 0)
-
-    def covariance(i, _):
-        at = pl.ds(pl.multiple_of(i * 128, 128), 128)
+def border(batch, await_rows, y_ref, yh, yl, ah, al, vinv, tref, wref, cross_ref, qref, inno, var):
+    corner = lax.broadcasted_iota(jnp.int32, (128, 128), 0) == lax.broadcasted_iota(jnp.int32, (128, 128), 1)
+    for s in range(3):
+        at = slice(128 * s, 128 * s + 128)
+        await_rows(s)
+
+        def centre(i, _):
+            rows = pl.ds(pl.multiple_of(s * 128 + i * 32, 32), 32)
+            y = y_ref[batch, rows, :]
+            mean = jnp.sum(y, axis=1, keepdims=True) * (1.0 / 1024.0)
+            yh[rows, :], yl[rows, :] = split(y - mean)
+            inno[rows, :] = inno[rows, :] - mean
+            return 0
+
+        lax.fori_loop(0, 4, centre, 0)
         high, low = yh[at, :], yl[at, :]
-        total = dot_t(high, yh[...]) + (dot_t(high, yl[...]) + dot_t(low, yh[...]))
-        row = lax.broadcasted_iota(jnp.int32, (128, 384), 0) + i * 128
-        col = lax.broadcasted_iota(jnp.int32, (128, 384), 1)
-        wide = jnp.concatenate([var[at, :]] * 3, axis=1)
-        cov[at, :] = total * (1.0 / 1023.0) + jnp.where(row == col, wide, 0.0)
-        return 0
-
-    lax.fori_loop(0, 3, covariance, 0)
-
-    def eliminate(k, _):
-        at = pl.ds(pl.multiple_of(k * 128, 128), 128)
-        inv = inverse128(cov[at, at])
-        row = lax.broadcasted_iota(jnp.int32, (128, 384), 0) + k * 128
-        col = lax.broadcasted_iota(jnp.int32, (128, 384), 1)
-        inside = (col >= k * 128) & (col < k * 128 + 128)
-        top = dot(inv, jnp.where(inside, jnp.where(row == col, 1.0, 0.0), cov[at, :]), HIGHEST)
-        for i in range(3):
-            part = slice(i * 128, i * 128 + 128)
-            cov[part, :] = jnp.where(inside, 0.0, cov[part, :]) - dot(cov[part, at], top, HIGHEST)
-        cov[at, :] = top
-        return 0
-
-    lax.fori_loop(0, 3, eliminate, 0)
-
-
-def gain_of(x_ref, yh, yl, ah, al, cov, inno):
+        upto = slice(0, 128 * s + 128)
+        total = dot_t(high, yh[upto, :]) + (dot_t(high, yl[upto, :]) + dot_t(low, yh[upto, :]))
+        c = [total[:, 128 * i : 128 * i + 128] * (1.0 / 1023.0) for i in range(s + 1)]
+        schur = c[s] + jnp.where(corner, var[at, :], 0.0)
+        if batch:
+            x = cross_of(ah, al, high, low)
+        if s == 0:
+            if batch:
+                cross_ref[:, 0:128] = x
+            vinv[0] = inverse128(schur)
+        elif s == 1:
+            t10 = dot(c[0], vinv[0], HIGHEST)
+            tref[...] = t10
+            schur = schur - dot_t(t10, c[0], HIGHEST)
+            if batch:
+                cross_ref[:, 128:256] = x - dot_t(cross_ref[:, 0:128], t10, HIGHEST)
+            vinv[1] = inverse128(schur)
+            if batch:
+                p1 = dot(cross_ref[:, 128:256], vinv[1], HIGHEST)
+                qref[:, 128:256] = p1
+                qref[:, 0:128] = dot(cross_ref[:, 0:128], vinv[0], HIGHEST) - dot(p1, t10, HIGHEST)
+        else:
+            t10 = tref[...]
+            t20 = dot(c[0], vinv[0], HIGHEST)
+            e21 = c[1] - dot_t(c[0], t10, HIGHEST)
+            t21 = dot(e21, vinv[1], HIGHEST)
+            schur = schur - (dot_t(t20, c[0], HIGHEST) + dot_t(t21, e21, HIGHEST))
+            wref[:, 0:128] = t20 - dot(t21, t10, HIGHEST)
+            wref[:, 128:256] = t21
+            if batch:
+                past = dot_t(cross_ref[:, 0:128], t20, HIGHEST) + dot_t(cross_ref[:, 128:256], t21, HIGHEST)
+                cross_ref[:, 256:384] = x - past
+            vinv[2] = inverse128(schur)
+
+
+def cross_of(ah, al, high, low):
+    a, b = ah[...], al[...]
+    return (dot_t(a, high) + (dot_t(a, low) + dot_t(b, high))) * (1.0 / 1023.0)
+
+
+def anomalies(x_ref, ah, al):
     def anomaly(i, _):
         at = pl.ds(pl.multiple_of(i * 32, 32), 32)
         x = x_ref[at, :]
@@ -256,17 +267,31 @@
         return 0
 
     lax.fori_loop(0, 8, anomaly, 0)
-    high, low = ah[...], al[...]
-    cross = (dot_t(high, yh[...]) + (dot_t(high, yl[...]) + dot_t(low, yh[...]))) * (1.0 / 1023.0)
-    gain = dot(cross, cov[...], HIGHEST)
-    return gain, dot(gain, inno[...], HIGHEST)
+
+
+def whole_gain(cross, vinv, tref, wref, gain_ref):
+    x0, x1, x2 = (cross[:, 128 * i : 128 * i + 128] for i in range(3))
+    t10, w0, w1 = tref[...], wref[:, 0:128], wref[:, 128:256]
+    x1 = x1 - dot_t(x0, t10, HIGHEST)
+    x2 = x2 - (dot_t(x0, w0, HIGHEST) + dot_t(cross[:, 128:256], w1, HIGHEST))
+    p0, p1 = dot(x0, vinv[0], HIGHEST), dot(x1, vinv[1], HIGHEST)
+    last = dot(x2, vinv[2], HIGHEST)
+    gain_ref[:, 256:384] = last
+    gain_ref[:, 128:256] = p1 - dot(last, w1, HIGHEST)
+    gain_ref[:, 0:128] = (p0 - dot(p1, t10, HIGHEST)) - dot(last, w0, HIGHEST)
+
+
+def last_gain(vinv, wref, cross_ref, qref, gain_ref):
+    last = dot(cross_ref[:, 256:384], vinv[2], HIGHEST)
+    gain_ref[:, 256:384] = last
+    gain_ref[:, 0:256] = qref[...] - dot(last, wref[...], HIGHEST)
 
 
 def whole_kernel(
     state_hbm, cell_hbm, val_hbm, var_hbm, nbr_ref, o_ref,
     state_ref, cell_ref, val_ref, var_ref,
     rows, sbuf, y_ref, xbuf, x_ref, x2_ref, rbuf, tbuf,
-    yh, yl, ah, al, cov, inno, var,
+    yh, yl, ah, al, vinv, tref, wref, cross_ref, qref, gain_ref, inno, var,
     load_sem, send_sem, recv_sem, xsend_sem, xrecv_sem, asend_sem, arecv_sem, osend_sem, orecv_sem,
 ):
     region, member, sides = place()
@@ -295,22 +320,28 @@
     sent = exchange(0, region, member, sides, nbr_ref, rows, sbuf, y_ref, send_sem, recv_sem)
     for q in range(8):
         xbuf[q] = state_ref[:, q, :].T
+    for d in range(1, 8):
+        other = lax.rem(member + d, 8)
+        copy = remote(xbuf.at[other], x_ref.at[:, columns(member)], xsend_sem.at[d], xrecv_sem.at[member], region, other)
+        copy.start()
+        sent.append(copy)
     x_ref[:, columns(member)] = xbuf[member]
     loads[2].wait()
     loads[3].wait()
     observed(0, patch, region, sides, nbr_ref, val_ref, var_ref, inno, var)
-    await_rows(0, member, sides, sbuf, y_ref, send_sem, recv_sem)
+
+    def first_rows(s):
+        await_side(0, s, member, sides, sbuf, y_ref, send_sem, recv_sem)
+
+    border(0, first_rows, y_ref, yh, yl, ah, al, vinv, tref, wref, cross_ref, qref, inno, var)
     for d in range(1, 8):
         other = lax.rem(member + d, 8)
-        copy = remote(xbuf.at[other], x_ref.at[:, columns(member)], xsend_sem.at[d], xrecv_sem.at[member], region, other)
-        copy.start()
-        sent.append(copy)
-    inverse_covariance(0, y_ref, yh, yl, cov, inno, var)
-    for d in range(1, 8):
-        other = lax.rem(member + d, 8)
         remote(xbuf.at[other], x_ref.at[:, columns(other)], xsend_sem.at[d], xrecv_sem.at[other], region, other).wait_recv()
 
-    gain, shift = gain_of(x_ref, yh, yl, ah, al, cov, inno)
+    anomalies(x_ref, ah, al)
+    whole_gain(cross_of(ah, al, yh[...], yl[...]), vinv, tref, wref, gain_ref)
+    gain = gain_ref[...]
+    shift = dot(gain, inno[...], HIGHEST)
     cell = jnp.sum(jnp.where(lane == patch, cell_ref[1], 0), axis=1, keepdims=True)
     picked = jnp.where(lane == cell, 1.0, 0.0)
     pshift = dot(picked, shift, HIGHEST)
@@ -333,15 +364,21 @@
         at = slice(i * 128, i * 128 + 128)
         h, l = yh[:, at], yl[:, at]
         x2_ref[:, at] = x_ref[:, at] + (shift + (dot(gh, h) + (dot(gh, l) + dot(gl, h))))
+    observed(1, patch, region, sides, nbr_ref, val_ref, var_ref, inno, var)
     for d in range(1, 8):
         other = lax.rem(member + d, 8)
         remote(rbuf.at[d], rows.at[1, other], asend_sem.at[d], arecv_sem.at[other], region, other).wait_recv()
 
     sent += exchange(1, region, member, sides, nbr_ref, rows, sbuf, y_ref, send_sem, recv_sem)
-    observed(1, patch, region, sides, nbr_ref, val_ref, var_ref, inno, var)
-    await_rows(1, member, sides, sbuf, y_ref, send_sem, recv_sem)
-    inverse_covariance(1, y_ref, yh, yl, cov, inno, var)
-    gain, shift = gain_of(x2_ref, yh, yl, ah, al, cov, inno)
+    anomalies(x2_ref, ah, al)
+
+    def later_rows(s):
+        await_side(1, s, member, sides, sbuf, y_ref, send_sem, recv_sem)
+
+    border(1, later_rows, y_ref, yh, yl, ah, al, vinv, tref, wref, cross_ref, qref, inno, var)
+    last_gain(vinv, wref, cross_ref, qref, gain_ref)
+    gain = gain_ref[...]
+    shift = dot(gain, inno[...], HIGHEST)
     gh, gl = split(-0.5 * gain)
     for d in (1, 2, 3, 4, 5, 6, 7, 0):
         other = lax.rem(member + d, 8)
@@ -386,7 +423,12 @@
             pltpu.VMEM((384, 1024), BF16),
             pltpu.VMEM((256, 1024), BF16),
             pltpu.VMEM((256, 1024), BF16),
-            pltpu.VMEM((384, 384), F32),
+            pltpu.VMEM((3, 128, 128), F32),
+            pltpu.VMEM((128, 128), F32),
+            pltpu.VMEM((128, 256), F32),
+            pltpu.VMEM((256, 384), F32),
+            pltpu.VMEM((256, 256), F32),
+            pltpu.VMEM((256, 384), F32),
             pltpu.VMEM((384, 128), F32),
             pltpu.VMEM((384, 128), F32),
             DMA((4,)),

time: 123 us -> 106 us (0.86)
  Pallas kernels: 120 us -> 103 us
    pallas_call x1, Pallas kernels: 120 us -> 103 us  [on_device(): pl.pallas_call(whole_kernel, out_shape=jax.ShapeDtypeStruct((8, 128, 256)...]
where the time goes in v3:
time: 106 us
  Pallas kernels  103 us (97%)
  local copies, waits for them, and re-layouts  2.81 us (3%)
    pallas_call x1, Pallas kernels, on_device(): pl.pallas_call(whole_kernel, out_shape=jax.ShapeDtypeStruct((8, 128, 256)...  103 us
    transpose x1, local copies, waits for them, and re-layouts, on_device(): return jnp.transpose(out, (1, 0, 2))  2.81 us

profile of v3, /device:TPU:1, one launch (start us, length us, event | category | flops | bytes accessed | tf_op | source)
XLA Modules:
  0.0 105.6 jit_solution(7252295070678529120)
XLA Ops:
  0.0 102.8 %whole.1 = f32[8,128,256]{2,1,0:T(8,128)} custom-call(f32[128,8,256]{2,1,0:T(8,128)} %state_hbm.1, s32[2,64,256]{2,1,0:T(8,128)} %bitcast.6, f32[2,64,256]{2,1,0:T(8,128)} %bitcast.7, f32[2,64,256]{2,1,0:T(8,128)} %bitcast.8, s32[5,256]{1,0:T(8,128)} %bitcast.9), custom_call_target="tpu_custom_call" | custom-call | tf_op jit(solution)/shard_map/whole/pallas_call | solution.py:404
  102.8 2.8 %copy.6 = f32[128,8,256]{2,1,0:T(8,128)} copy(f32[128,8,256]{2,0,1:T(8,128)} %bitcast.5) | data formatting | bytes 2097152 | tf_op jit(solution)/shard_map/transpose | solution.py:455

commit v4 on v3

--- a/solution.py
+++ b/solution.py
@@ -89,6 +89,48 @@
         return pltpu.roll(jnp.concatenate([fresh, top], axis=0), 96, 1)
 
     return lax.fori_loop(0, 4, strip, block)
+
+
+def inverse128_unrolled(block):
+    lane = lax.broadcasted_iota(jnp.int32, TILE, 1)
+    sub = lax.broadcasted_iota(jnp.int32, TILE, 0)
+    lanes = lax.broadcasted_iota(jnp.int32, (96, 128), 1)
+    tiles = [block[8 * i : 8 * i + 8, :] for i in range(16)]
+    for s in range(4):
+        mine = list(range(4 * s, 4 * s + 4))
+        others = [i for i in range(16) if i not in mine]
+        old = jnp.concatenate([tiles[i] for i in others], axis=0)
+        for t in mine:
+            cols = {i: [spread_tile(tiles[i][:, 8 * t + k : 8 * t + k + 1]) for k in range(8)] for i in mine}
+            e = [[spread_tile(cols[t][j][k : k + 1, :]) if j <= k else None for j in range(8)] for k in range(8)]
+            inside = (lane >= 8 * t) & (lane < 8 * t + 8)
+            rows = [
+                jnp.where(lane == 8 * t + k, 1.0, jnp.where(inside, 0.0, spread_tile(tiles[t][k : k + 1, :])))
+                for k in range(8)
+            ]
+            new = solve8(e, rows)
+            for i in mine:
+                if i == t:
+                    u = new[0]
+                    for k in range(1, 8):
+                        u = jnp.where(sub == k, new[k], u)
+                else:
+                    u = jnp.where(inside, 0.0, tiles[i])
+                    p = [cols[i][k] * new[k] for k in range(8)]
+                    u = u - (((p[0] + p[1]) + (p[2] + p[3])) + ((p[4] + p[5]) + (p[6] + p[7])))
+                tiles[i] = u
+        low, high = 32 * s, 32 * s + 32
+        parts = [jnp.concatenate([tiles[i] for i in mine], axis=0)]
+        if low:
+            parts.insert(0, jnp.zeros((low, 128), F32))
+        if high < 128:
+            parts.append(jnp.zeros((128 - high, 128), F32))
+        strip = jnp.concatenate(parts, axis=0)
+        inside = (lanes >= low) & (lanes < high)
+        fresh = jnp.where(inside, 0.0, old) - dot(jnp.where(inside, old, 0.0), strip, HIGHEST)
+        for q, i in enumerate(others):
+            tiles[i] = fresh[8 * q : 8 * q + 8]
+    return jnp.concatenate(tiles, axis=0)
 
 
 def linked(nbr_ref, patch, home):
@@ -205,6 +247,7 @@
 
 def border(batch, await_rows, y_ref, yh, yl, ah, al, vinv, tref, wref, cross_ref, qref, inno, var):
     corner = lax.broadcasted_iota(jnp.int32, (128, 128), 0) == lax.broadcasted_iota(jnp.int32, (128, 128), 1)
+    inverse = inverse128_unrolled if batch else inverse128
     for s in range(3):
         at = slice(128 * s, 128 * s + 128)
         await_rows(s)
@@ -228,14 +271,14 @@
         if s == 0:
             if batch:
                 cross_ref[:, 0:128] = x
-            vinv[0] = inverse128(schur)
+            vinv[0] = inverse(schur)
         elif s == 1:
             t10 = dot(c[0], vinv[0], HIGHEST)
             tref[...] = t10
             schur = schur - dot_t(t10, c[0], HIGHEST)
             if batch:
                 cross_ref[:, 128:256] = x - dot_t(cross_ref[:, 0:128], t10, HIGHEST)
-            vinv[1] = inverse128(schur)
+            vinv[1] = inverse(schur)
             if batch:
                 p1 = dot(cross_ref[:, 128:256], vinv[1], HIGHEST)
                 qref[:, 128:256] = p1
@@ -251,22 +294,12 @@
             if batch:
                 past = dot_t(cross_ref[:, 0:128], t20, HIGHEST) + dot_t(cross_ref[:, 128:256], t21, HIGHEST)
                 cross_ref[:, 256:384] = x - past
-            vinv[2] = inverse128(schur)
+            vinv[2] = inverse(schur)
 
 
 def cross_of(ah, al, high, low):
     a, b = ah[...], al[...]
     return (dot_t(a, high) + (dot_t(a, low) + dot_t(b, high))) * (1.0 / 1023.0)
-
-
-def anomalies(x_ref, ah, al):
-    def anomaly(i, _):
-        at = pl.ds(pl.multiple_of(i * 32, 32), 32)
-        x = x_ref[at, :]
-        ah[at, :], al[at, :] = split(x - jnp.sum(x, axis=1, keepdims=True) * (1.0 / 1024.0))
-        return 0
-
-    lax.fori_loop(0, 8, anomaly, 0)
 
 
 def whole_gain(cross, vinv, tref, wref, gain_ref):
@@ -334,23 +367,29 @@
         await_side(0, s, member, sides, sbuf, y_ref, send_sem, recv_sem)
 
     border(0, first_rows, y_ref, yh, yl, ah, al, vinv, tref, wref, cross_ref, qref, inno, var)
-    for d in range(1, 8):
-        other = lax.rem(member + d, 8)
-        remote(xbuf.at[other], x_ref.at[:, columns(other)], xsend_sem.at[d], xrecv_sem.at[other], region, other).wait_recv()
-
-    anomalies(x_ref, ah, al)
-    whole_gain(cross_of(ah, al, yh[...], yl[...]), vinv, tref, wref, gain_ref)
+    for d in range(8):
+        other = lax.rem(member + 8 - d, 8)
+        at = columns(other)
+        if d:
+            remote(xbuf.at[other], x_ref.at[:, at], xsend_sem.at[d], xrecv_sem.at[other], region, other).wait_recv()
+        high, low = split(x_ref[:, at])
+        ah[:, at], al[:, at] = high, low
+        part = dot_t(high, yh[:, at]) + (dot_t(high, yl[:, at]) + dot_t(low, yh[:, at]))
+        cross_ref[...] = cross_ref[...] + part if d else part
+
+    whole_gain(cross_ref[...] * (1.0 / 1023.0), vinv, tref, wref, gain_ref)
     gain = gain_ref[...]
     shift = dot(gain, inno[...], HIGHEST)
     cell = jnp.sum(jnp.where(lane == patch, cell_ref[1], 0), axis=1, keepdims=True)
     picked = jnp.where(lane == cell, 1.0, 0.0)
+    chosen = picked.astype(BF16)
     pshift = dot(picked, shift, HIGHEST)
     ph, pl_ = split(dot(picked, -0.5 * gain, HIGHEST))
-    for d in range(8):
+    for d in (1, 2, 3, 4, 5, 6, 7, 0):
         other = lax.rem(member + d, 8)
         at = columns(other)
         h, l = yh[:, at], yl[:, at]
-        r = dot(picked, x_ref[:, at], HIGHEST) + (pshift + (dot(ph, h) + (dot(ph, l) + dot(pl_, h))))
+        r = (dot(chosen, ah[:, at]) + dot(chosen, al[:, at])) + (pshift + (dot(ph, h) + (dot(ph, l) + dot(pl_, h))))
         rbuf[d] = r
         y_ref[1, 0:OBS, at] = r
         if d == 0:
@@ -363,14 +402,15 @@
     for i in range(8):
         at = slice(i * 128, i * 128 + 128)
         h, l = yh[:, at], yl[:, at]
-        x2_ref[:, at] = x_ref[:, at] + (shift + (dot(gh, h) + (dot(gh, l) + dot(gl, h))))
+        x = x_ref[:, at] + (shift + (dot(gh, h) + (dot(gh, l) + dot(gl, h))))
+        x2_ref[:, at] = x
+        ah[:, at], al[:, at] = split(x)
     observed(1, patch, region, sides, nbr_ref, val_ref, var_ref, inno, var)
     for d in range(1, 8):
         other = lax.rem(member + d, 8)
         remote(rbuf.at[d], rows.at[1, other], asend_sem.at[d], arecv_sem.at[other], region, other).wait_recv()
 
     sent += exchange(1, region, member, sides, nbr_ref, rows, sbuf, y_ref, send_sem, recv_sem)
-    anomalies(x2_ref, ah, al)
 
     def later_rows(s):
         await_side(1, s, member, sides, sbuf, y_ref, send_sem, recv_sem)

time: 106 us -> 106 us (level)
  no operation moved by 1% of the time
where the time goes in v4:
time: 106 us; the launch traced here: 105 us
  Pallas kernels  102 us (96%)
  local copies, waits for them, and re-layouts  2.81 us (3%)
    pallas_call x1, Pallas kernels, on_device(): pl.pallas_call(whole_kernel, out_shape=jax.ShapeDtypeStruct((8, 128, 256)...  102 us
    transpose x1, local copies, waits for them, and re-layouts, on_device(): return jnp.transpose(out, (1, 0, 2))  2.81 us

profile of v4, /device:TPU:1, one launch (start us, length us, event | category | flops | bytes accessed | tf_op | source)
XLA Modules:
  0.0 104.7 jit_solution(16604647498290643361)
XLA Ops:
  0.0 101.9 %whole.1 = f32[8,128,256]{2,1,0:T(8,128)} custom-call(f32[128,8,256]{2,1,0:T(8,128)} %state_hbm.1, s32[2,64,256]{2,1,0:T(8,128)} %bitcast.6, f32[2,64,256]{2,1,0:T(8,128)} %bitcast.7, f32[2,64,256]{2,1,0:T(8,128)} %bitcast.8, s32[5,256]{1,0:T(8,128)} %bitcast.9), custom_call_target="tpu_custom_call" | custom-call | tf_op jit(solution)/shard_map/whole/pallas_call | solution.py:444
  101.9 2.8 %copy.6 = f32[128,8,256]{2,1,0:T(8,128)} copy(f32[128,8,256]{2,0,1:T(8,128)} %bitcast.5) | data formatting | bytes 2097152 | tf_op jit(solution)/shard_map/transpose | solution.py:495

commit v5 on v4

--- a/solution.py
+++ b/solution.py
@@ -183,20 +183,20 @@
     return OBS if batch and s == 0 else 0
 
 
-def exchange(batch, region, member, sides, nbr_ref, rows, sbuf, y_ref, send_sem, recv_sem):
+def exchange(batch, picks, member, sides, rows, sbuf, y_ref, send_sem, recv_sem):
     sent = []
     for s in range(3):
         start = start_of(batch, s)
         for d in range(8):
             other = lax.rem(member + d, 8)
-            first, _, last, _ = linked(nbr_ref, sides[s] * 8 + other, region)
+            first, last = picks[s][d]
             if s == 0:
                 if batch == 0:
                     sbuf[batch, s, d, 0:OBS, :] = rows[batch, other]
-                sbuf[batch, s, d, OBS : 2 * OBS, :] = rows[batch, first & 7]
+                sbuf[batch, s, d, OBS : 2 * OBS, :] = rows[batch, first]
             else:
-                sbuf[batch, s, d, 0:OBS, :] = rows[batch, first & 7]
-                sbuf[batch, s, d, OBS : 2 * OBS, :] = rows[batch, last & 7]
+                sbuf[batch, s, d, 0:OBS, :] = rows[batch, first]
+                sbuf[batch, s, d, OBS : 2 * OBS, :] = rows[batch, last]
             if s == 0 and d == 0:
                 y_ref[batch, start : 2 * OBS, columns(member)] = sbuf[batch, 0, 0, start : 2 * OBS, :]
                 continue
@@ -321,9 +321,9 @@
 
 
 def whole_kernel(
-    state_hbm, cell_hbm, val_hbm, var_hbm, nbr_ref, o_ref,
+    state_hbm, cell_hbm, val_hbm, var_hbm, nbr_ref, out_ref,
     state_ref, cell_ref, val_ref, var_ref,
-    rows, sbuf, y_ref, xbuf, x_ref, x2_ref, rbuf, tbuf,
+    rows, sbuf, y_ref, xbuf, x_ref, x2_ref, rbuf, tbuf, o_ref,
     yh, yl, ah, al, vinv, tref, wref, cross_ref, qref, gain_ref, inno, var,
     load_sem, send_sem, recv_sem, xsend_sem, xrecv_sem, asend_sem, arecv_sem, osend_sem, orecv_sem,
 ):
@@ -342,6 +342,11 @@
     barrier = pltpu.get_barrier_semaphore()
     for peer in peers:
         pl.semaphore_signal(barrier, inc=1, device_id=peer, device_id_type=MESH)
+    picks = [[], [], []]
+    for s in range(3):
+        for d in range(8):
+            first, _, last, _ = linked(nbr_ref, sides[s] * 8 + lax.rem(member + d, 8), region)
+            picks[s].append((first & 7, last & 7))
     loads[0].wait()
     loads[1].wait()
     for q in range(8):
@@ -350,7 +355,7 @@
         rows[0, q] = dot_t(picked, state_ref[:, q, :], HIGHEST)
     pl.semaphore_wait(barrier, len(peers))
 
-    sent = exchange(0, region, member, sides, nbr_ref, rows, sbuf, y_ref, send_sem, recv_sem)
+    sent = exchange(0, picks, member, sides, rows, sbuf, y_ref, send_sem, recv_sem)
     for q in range(8):
         xbuf[q] = state_ref[:, q, :].T
     for d in range(1, 8):
@@ -379,12 +384,12 @@
 
     whole_gain(cross_ref[...] * (1.0 / 1023.0), vinv, tref, wref, gain_ref)
     gain = gain_ref[...]
-    shift = dot(gain, inno[...], HIGHEST)
     cell = jnp.sum(jnp.where(lane == patch, cell_ref[1], 0), axis=1, keepdims=True)
     picked = jnp.where(lane == cell, 1.0, 0.0)
     chosen = picked.astype(BF16)
-    pshift = dot(picked, shift, HIGHEST)
-    ph, pl_ = split(dot(picked, -0.5 * gain, HIGHEST))
+    pgain = dot(picked, gain, HIGHEST)
+    pshift = dot(pgain, inno[...], HIGHEST)
+    ph, pl_ = split(-0.5 * pgain)
     for d in (1, 2, 3, 4, 5, 6, 7, 0):
         other = lax.rem(member + d, 8)
         at = columns(other)
@@ -398,6 +403,7 @@
         copy = remote(rbuf.at[d], rows.at[1, member], asend_sem.at[d], arecv_sem.at[member], region, other)
         copy.start()
         sent.append(copy)
+    shift = dot(gain, inno[...], HIGHEST)
     gh, gl = split(-0.5 * gain)
     for i in range(8):
         at = slice(i * 128, i * 128 + 128)
@@ -410,7 +416,7 @@
         other = lax.rem(member + d, 8)
         remote(rbuf.at[d], rows.at[1, other], asend_sem.at[d], arecv_sem.at[other], region, other).wait_recv()
 
-    sent += exchange(1, region, member, sides, nbr_ref, rows, sbuf, y_ref, send_sem, recv_sem)
+    sent += exchange(1, picks, member, sides, rows, sbuf, y_ref, send_sem, recv_sem)
 
     def later_rows(s):
         await_side(1, s, member, sides, sbuf, y_ref, send_sem, recv_sem)
@@ -432,9 +438,13 @@
         copy = remote(tbuf.at[d], o_ref.at[member], osend_sem.at[d], orecv_sem.at[member], region, other)
         copy.start()
         sent.append(copy)
-    for d in range(1, 8):
-        other = lax.rem(member + d, 8)
-        remote(tbuf.at[d], o_ref.at[other], osend_sem.at[d], orecv_sem.at[other], region, other).wait_recv()
+    for p in range(8):
+
+        @pl.when(member != p)
+        def _():
+            remote(tbuf.at[1], o_ref.at[p], osend_sem.at[1], orecv_sem.at[p], region, p).wait_recv()
+
+        out_ref[:, p, :] = o_ref[p]
     for copy in sent:
         copy.wait_send()
 
@@ -443,7 +453,7 @@
     small = pltpu.VMEM((2, OBS, 256), F32)
     out = pl.pallas_call(
         whole_kernel,
-        out_shape=jax.ShapeDtypeStruct((8, 128, 256), F32),
+        out_shape=jax.ShapeDtypeStruct((128, 8, 256), F32),
         in_specs=[ANY] * 4 + [SMEM],
         out_specs=VMEM,
         scratch_shapes=[
@@ -458,6 +468,7 @@
             pltpu.VMEM((256, 1024), F32),
             pltpu.VMEM((256, 1024), F32),
             pltpu.VMEM((8, OBS, 128), F32),
+            pltpu.VMEM((8, 128, 256), F32),
             pltpu.VMEM((8, 128, 256), F32),
             pltpu.VMEM((384, 1024), BF16),
             pltpu.VMEM((384, 1024), BF16),
@@ -492,7 +503,7 @@
         jnp.transpose(obs_var, (1, 2, 0)),
         jnp.transpose(neighbours, (1, 0)),
     )
-    return jnp.transpose(out, (1, 0, 2))
+    return out
 
 
 def solution(mesh):

time: 106 us -> 105 us (level)
    transpose x1 -> x0, local copies, waits for them, and re-layouts: 2.81 us -> none  [on_device(): return jnp.transpose(out, (1, 0, 2))]
    unnamed x0 -> x1, local copies, waits for them, and re-layouts: none -> 2.26 us
where the time goes in v5:
time: 105 us; the launch traced here: 104 us
  Pallas kernels  101 us (96%)
  local copies, waits for them, and re-layouts  2.26 us (2%)
    pallas_call x1, Pallas kernels, on_device(): pl.pallas_call(whole_kernel, out_shape=jax.ShapeDtypeStruct((128, 8, 256)...  101 us
    unnamed x1, local copies, waits for them, and re-layouts  2.26 us

profile of v5, /device:TPU:1, one launch (start us, length us, event | category | flops | bytes accessed | tf_op | source)
XLA Modules:
  0.0 103.6 jit_solution(4342935931544564317)
XLA Ops:
  0.0 101.4 %whole.1 = f32[128,8,256]{2,1,0:T(8,128)} custom-call(f32[128,8,256]{2,1,0:T(8,128)} %state_hbm.1, s32[2,64,256]{2,1,0:T(8,128)} %bitcast.4, f32[2,64,256]{2,1,0:T(8,128)} %bitcast.5, f32[2,64,256]{2,1,0:T(8,128)} %bitcast.6, s32[5,256]{1,0:T(8,128)} %bitcast.7), custom_call_target="tpu_custom_call" | custom-call | tf_op jit(solution)/shard_map/whole/pallas_call | solution.py:454
  101.4 2.3 %copy.7 = f32[128,8,256]{2,1,0:T(8,128)} copy(f32[128,8,256]{2,1,0:T(8,128)} %whole.1) | data formatting | bytes 2097152

commit v6 on v5

--- a/solution.py
+++ b/solution.py
@@ -352,7 +352,10 @@
     for q in range(8):
         cell = jnp.sum(jnp.where(lane == region * 8 + q, cell_ref[0], 0), axis=1, keepdims=True)
         picked = jnp.where(lane == cell, 1.0, 0.0)
-        rows[0, q] = dot_t(picked, state_ref[:, q, :], HIGHEST)
+        chosen, x = picked.astype(BF16), state_ref[:, q, :]
+        high = x.astype(BF16)
+        middle, low = split(x - high.astype(F32))
+        rows[0, q] = (dot_t(chosen, high) + dot_t(chosen, middle)) + dot_t(chosen, low)
     pl.semaphore_wait(barrier, len(peers))
 
     sent = exchange(0, picks, member, sides, rows, sbuf, y_ref, send_sem, recv_sem)

time: 105 us -> 112 us (1.067)
  the two profiles are of different devices: /device:TPU:1 before, /device:TPU:231 now
where the time goes in v6:
time: 112 us; the launch traced here: 111 us
  Pallas kernels  109 us (97%)
  local copies, waits for them, and re-layouts  2.26 us (2%)
    pallas_call x1, Pallas kernels, on_device(): pl.pallas_call(whole_kernel, out_shape=jax.ShapeDtypeStruct((128, 8, 256)...  109 us
    unnamed x1, local copies, waits for them, and re-layouts  2.26 us

profile of v6, /device:TPU:231, one launch (start us, length us, event | category | flops | bytes accessed | tf_op | source)
XLA Modules:
  0.0 111.4 jit_solution(14029437749659572385)
XLA Ops:
  0.0 109.1 %whole.1 = f32[128,8,256]{2,1,0:T(8,128)} custom-call(f32[128,8,256]{2,1,0:T(8,128)} %state_hbm.1, s32[2,64,256]{2,1,0:T(8,128)} %bitcast.4, f32[2,64,256]{2,1,0:T(8,128)} %bitcast.5, f32[2,64,256]{2,1,0:T(8,128)} %bitcast.6, s32[5,256]{1,0:T(8,128)} %bitcast.7), custom_call_target="tpu_custom_call" | custom-call | tf_op jit(solution)/shard_map/whole/pallas_call | solution.py:457
  109.1 2.3 %copy.7 = f32[128,8,256]{2,1,0:T(8,128)} copy(f32[128,8,256]{2,1,0:T(8,128)} %whole.1) | data formatting | bytes 2097152
